TPU v7x, 256 devices: a whole 4x4x8 slice. The times are simulated.
256 devices in a mesh: group: 64 (over x, z, core), batch: 4 (over y).
Axes of the slice: x: 4, y: 4, z: 8, core: 2. Of those that a mesh axis runs over, the one named last changes fastest.
Arguments:
- mixed_input: bfloat16 [65536, 2816], P(('batch', 'group')), parts along dimension 0, may hold values from -6 to 6
- conv_weight: float32 [4, 2816], replicated, may hold values from -3 to 3
- conv_bias: float32 [2816], replicated, may hold values from -3 to 3
- gate_input: bfloat16 [65536, 2560], P(('batch', 'group')), parts along dimension 0, may hold values from -6 to 6
- log_decay: float32 [40, 65536], P(None, ('batch', 'group')), parts along dimension 1, may hold values from -0.76 to 0, as said below
- level_weights: float32 [40, 20, 65536], P(None, None, ('batch', 'group')), parts along dimension 2, may hold values from 0.2 to 2
- skip_gain: float32 [40], replicated, may hold values from 0.3 to 3
- norm_gain: float32 [2560], replicated, may hold values from 0.25 to 1.75
- seg_lengths: int32 [12], P('batch'), parts along dimension 0, may hold values from 1 to 10240, 16384 in all
Outputs:
- output: bfloat16 [65536, 2560], P(('batch', 'group')), parts along dimension 0
There are 4 independent parts, one for each index of `batch`. A program takes and returns all parts, laid end to end along the dimension named above; an argument that names none is the same for every part. Nothing has to cross between parts.
Inputs may be any that keep to these rules, and one draw needn't show every extreme that they name: `seg_lengths`: the recordings' lengths in order; they sum to 16384 and the longest is exactly 10240. `log_decay`: every entry is negative.
All inputs are finite; a program needn't handle non-finite values.
Results may differ from a plain program's by a relative error of at most 0.0034.
Values may be sent and summed in bfloat16 or wider, within the bound.
A program may use at most 128 MiB of HBM per device.

v0:
```python
import jax
import jax.numpy as jnp
from jax import lax
from jax.sharding import PartitionSpec as P

eps_norm = 1e-05


def shifted(array, axis, by):
    peers = lax.axis_size(axis)
    pairs = [(i, i + by) for i in range(peers) if 0 <= i + by < peers]
    return lax.ppermute(array, axis, pairs)


def partner(value, axis, apart):
    mask = 2**apart
    pairs = [(source, source ^ mask) for source in range(lax.axis_size(axis))]
    return lax.ppermute(value, axis, pairs)


def segment_of(positions, seg_lengths):
    bounds = jnp.cumsum(seg_lengths)[:-1]
    found = jnp.sum((positions[:, None] >= bounds[None, :]).astype(jnp.int32), axis=1)
    return jnp.where(positions >= 0, found, -1)


def pair_levels(count, low_bits):
    index = jnp.arange(count, dtype=jnp.int32)
    diff = jnp.bitwise_xor(index[:, None], index[None, :])
    levels = jnp.zeros((count, count), jnp.int32)
    for bit_index in range(low_bits):
        levels = levels + (diff >= 2**bit_index).astype(jnp.int32)
    return levels


def convolve(rows, segs, conv_weight, conv_bias, taps):
    count = rows.shape[0] - (taps - 1)
    total = jnp.zeros((count, rows.shape[1]), jnp.float32) + conv_bias[None, :]
    for tap in range(taps):
        begin = taps - 1 - tap
        piece = rows[begin : begin + count].astype(jnp.float32)
        same = (segs[begin : begin + count] == segs[taps - 1 :]).astype(jnp.float32)
        total = total + conv_weight[tap][None, :] * piece * same[:, None]
    return jax.nn.silu(total)


def head_block():
    for block_try in (8, 5, 4, 2):
        return block_try
    return 1


def per_device(
    mixed_input,
    conv_weight,
    conv_bias,
    gate_input,
    log_decay,
    level_weights,
    skip_gain,
    norm_gain,
    seg_lengths,
):
    tok_rows = mixed_input.shape[0]
    width = gate_input.shape[1]
    head_count = log_decay.shape[0]
    head_dim = width // head_count
    state_dim = (mixed_input.shape[1] - width) // 2
    taps = conv_weight.shape[0]
    low_bits = tok_rows.bit_length() - 1
    group_count = lax.axis_size("group")
    high_bits = group_count.bit_length() - 1
    group_index = lax.axis_index("group")
    first_pos = group_index * tok_rows
    positions = first_pos + jnp.arange(tok_rows, dtype=jnp.int32)
    segments = segment_of(positions, seg_lengths)
    rim_segs = segment_of(
        first_pos - (taps - 1) + jnp.arange(taps - 1, dtype=jnp.int32), seg_lengths
    )
    rim_rows = shifted(mixed_input[tok_rows - (taps - 1) :], "group", 1)
    activated = convolve(
        jnp.concatenate([rim_rows, mixed_input], axis=0),
        jnp.concatenate([rim_segs, segments], axis=0),
        conv_weight,
        conv_bias,
        taps,
    )
    xs = activated[:, :width].astype(jnp.bfloat16)
    keys = activated[:, width : width + state_dim].astype(jnp.bfloat16)
    queries = activated[:, width + state_dim :].astype(jnp.bfloat16)
    cum = jnp.cumsum(log_decay, axis=1)
    prev_seg = segment_of(jnp.reshape(first_pos - 1, (1,)), seg_lengths)[0]
    entry = jnp.exp(cum) * (segments == prev_seg).astype(jnp.float32)[None, :]
    same_end = (segments == segments[-1]).astype(jnp.float32)
    end_weight = jnp.exp(cum[:, -1:] - cum) * same_end[None, :]
    scaled = (
        (xs.astype(jnp.float32).reshape(tok_rows, head_count, head_dim) * end_weight.T[:, :, None])
        .astype(jnp.bfloat16)
        .reshape(tok_rows, width)
    )
    end_state = lax.dot_general(
        keys, scaled, (((0,), (0,)), ((), ())), preferred_element_type=jnp.float32
    )
    through = jnp.exp(cum[:, -1]) * (segments[-1] == prev_seg).astype(jnp.float32)
    through_cols = jnp.repeat(through, head_dim)
    scores = jnp.dot(queries, keys.T, preferred_element_type=jnp.float32)
    pair_level = pair_levels(tok_rows, low_bits)
    row_ids = jnp.arange(tok_rows, dtype=jnp.int32)
    valid = (row_ids[None, :] <= row_ids[:, None]) & (segments[:, None] == segments[None, :])
    per_block = head_block()
    pieces = []
    for block_start in range(0, head_count, per_block):
        cum_block = cum[block_start : block_start + per_block]
        gap = jnp.where(valid[None], cum_block[:, :, None] - cum_block[:, None, :], 0.0)
        decay = jnp.exp(gap) * valid[None].astype(jnp.float32)
        picked = jnp.zeros_like(decay)
        for level_index in range(low_bits + 1):
            picked = jnp.where(
                pair_level[None] == level_index,
                level_weights[block_start : block_start + per_block, level_index, :, None],
                picked,
            )
        mixing = (scores[None] * picked * decay).astype(jnp.bfloat16)
        values = xs[:, block_start * head_dim : (block_start + per_block) * head_dim].reshape(
            tok_rows, per_block, head_dim
        )
        pieces.append(
            jnp.einsum("hts,shp->thp", mixing, values, preferred_element_type=jnp.float32)
        )
    local_part = jnp.concatenate(pieces, axis=1)
    kept = []
    running = end_state
    block_total = through_cols
    before = jnp.ones_like(through_cols)
    for bit_index in range(high_bits):
        far_state, far_total = partner((running, block_total), "group", bit_index)
        on_top = group_index // 2**bit_index % 2 == 1
        level_state = jnp.where(on_top, far_state * before[None, :], 0.0)
        kept.append(level_state)
        if bit_index + 1 < high_bits:
            running = jnp.where(
                on_top,
                far_state * block_total[None, :] + running,
                running * far_total[None, :] + far_state,
            )
            before = jnp.where(on_top, far_total * before, before)
            block_total = block_total * far_total
    level_total = len(kept)
    stacked = jnp.stack(kept, axis=0).astype(jnp.bfloat16)
    read = jnp.einsum("tn,lnw->tlw", queries, stacked, preferred_element_type=jnp.float32)
    factor = level_weights[:, low_bits + 1 : low_bits + 1 + level_total, :] * entry[:, None, :]
    shaped = read.reshape(tok_rows, level_total, head_count, head_dim)
    far_part = jnp.sum(shaped * jnp.transpose(factor, (2, 1, 0))[:, :, :, None], axis=1)
    mixed_sum = (
        local_part
        + far_part
        + skip_gain[None, :, None] * xs.astype(jnp.float32).reshape(tok_rows, head_count, head_dim)
    )
    flat = mixed_sum.reshape(tok_rows, width)
    gated = flat * jax.nn.silu(gate_input.astype(jnp.float32))
    scale = lax.rsqrt(jnp.mean(gated * gated, axis=1, keepdims=True) + eps_norm)
    return (gated * scale * norm_gain[None, :]).astype(jnp.bfloat16)


def solution(mesh):
    in_specs = (
        P(("batch", "group"), None),
        P(),
        P(),
        P(("batch", "group"), None),
        P(None, ("batch", "group")),
        P(None, None, ("batch", "group")),
        P(),
        P(),
        P("batch"),
    )
    out_specs = P(("batch", "group"), None)
    return jax.shard_map(
        per_device, mesh=mesh, in_specs=in_specs, out_specs=out_specs, check_vma=False
    )
```

profile of v0, /device:TPU:16, one launch (start us, length us, event | category | flops | bytes accessed | tf_op | source)
XLA Modules:
  0.0 282.9 jit_solution(3220069178034483166)
XLA Ops:
  0.0 0.8 slice.245
  0.8 1.7 collective-permute-start
  2.6 0.8 reduce-window.10
  3.4 0.6 slice_bitcast_fusion.50
  4.8 0.6 slice.316
  5.4 0.6 reduce-window.11
  6.0 0.2 slice_reduce_fusion
  6.3 0.2 slice_reduce_fusion.1
  7.3 2.2 collective-permute-start.2
  9.8 0.7 compare_convert_fusion.6
  10.5 1.1 slice_reduce_fusion.5
  11.7 0.1 broadcast_compare_fusion.7
  11.8 0.2 mul.430
  12.0 2.1 copy.46
  14.1 6.0 %multiply_convert_fusion = bf16[256,2816]{1,0:T(8,128)(2,1)S(1)} fusion(bf16[256,2816]{1,0:T(8,128)(2,1)} %param.9, bf16[3,2816]{1,0:T(4,128)(2,1)S(1)} %collective-permute-done, f32[256]{0:T(256)S(1)} %get-tuple-element.76, f32[2816]{0:T(1024)S(1)} %get-tuple-element.7, f32[256]{0:T(256)S(1)} %get-tuple-element.77, f32[2816]{0:T(1024)S(1)} %get-tuple-element.8, ...), kind=kLoop, calls=%fused_computation.5 | loop fusion | flops 20905984 | bytes 2959872 | tf_op jit(solution)/shard_map/convert.14
  20.2 1.6 fusion.8
  21.7 0.8 broadcast_compare_fusion.1
  22.5 0.6 slice_bitcast_fusion
  23.1 0.6 slice_bitcast_fusion.49
  23.7 0.7 slice_bitcast_fusion.5
  24.4 0.7 slice_bitcast_fusion.13
  25.2 0.8 broadcast_compare_fusion.5
  25.9 2.7 add_select_fusion.4
  28.6 1.9 collective-permute-start.3
  30.6 0.8 broadcast_compare_fusion.3
  31.4 0.7 mul.482
  32.1 6.8 %mul.478 = f32[256,6,40,64]{0,3,2,1:T(8,128)} broadcast(f32[256,6,40]{0,2,1:T(8,128)S(1)} %multiply_bitcast_fusion), dimensions={0,1,2} | broadcast | bytes 15974400 | tf_op jit(solution)/shard_map/mul | solution.py:153
  38.9 15.7 %copy.47 = f32[256,6,2560]{2,0,1:T(8,128)} copy(f32[256,6,2560]{0,2,1:T(8,128)} %bitcast.184) | data formatting | bytes 31457280 | tf_op jit(solution)/shard_map/mul | solution.py:153
  54.5 0.9 fusion.156
  55.5 0.1 collective-permute-start.4
  55.6 0.9 fusion.173
  56.5 1.8 copy.39
  58.3 0.2 fusion.159
  58.5 5.3 %fusion.14 = f32[256,40,64]{0,2,1:T(8,128)} fusion(bf16[256,8,64]{0,2,1:T(8,128)(2,1)} %bitcast.190, f32[256,256]{1,0:T(8,128)} %get-tuple-element.80, f32[8,256]{1,0:T(8,128)} %get-tuple-element.74, f32[8,256]{1,0:T(8,128)} %get-tuple-element.59, f32[8,256]{1,0:T(8,128)} %get-tuple-element.60, f32[8,256]{1,0:T(8,128)S(1)} %get-tuple-element.62, ...), kind=kOutput, calls=%fused_computation.45 | convolution fusion | flops 74973184 | bytes 2056192 | tf_op jit(solution)/shard_map/hts,shp->thp/dot_general | solution.py:128
  63.8 1.8 copy.41
  65.6 1.8 copy.42
  67.6 3.1 %add_select_fusion.3 = f32[128,2560]{1,0:T(8,128)} fusion(f32[128,2560]{1,0:T(8,128)} %collective-permute-done.3, f32[128,2560]{1,0:T(8,128)} %add_select_fusion.4, f32[2560]{0:T(1024)S(1)} %collective-permute-done.4, f32[2560]{0:T(1024)S(1)} %mul.442, pred[]{:T(512)S(6)} %eq.275), kind=kLoop, calls=%fused_computation.32 | loop fusion | flops 1638400 | bytes 3952641 | tf_op jit(solution)/shard_map/jit(_where)/select_n | solution.py:141
  70.7 4.4 %collective-permute-start.5 = (f32[128,2560]{1,0:T(8,128)}, f32[128,2560]{1,0:T(8,128)}, u32[]{:S(2)}, u32[]{:S(2)}) collective-permute-start(f32[128,2560]{1,0:T(8,128)} %add_select_fusion.3), channel_id=1, source_target_pairs={{0,16},{4,20},{8,24},{12,28},{16,0},{20,4},{24,8},{28,12},{32,48},... | collective-permute-start | bytes 3932168 | tf_op jit(solution)/shard_map/ppermute | solution.py:18
  75.3 4.1 %fusion.13 = f32[256,40,64]{0,2,1:T(8,128)} fusion(f32[256,40,64]{0,2,1:T(8,128)} %fusion.14, bf16[256,8,64]{0,2,1:T(8,128)(2,1)S(1)} %bitcast.188, f32[8,256]{1,0:T(8,128)S(1)} %copy-done.42, f32[8,256]{1,0:T(8,128)S(1)} %copy-done.52, f32[8,256]{1,0:T(8,128)S(1)} %copy-done.53, f32[8,256]{1,0:T(8,128)S(1)} %copy-done.54, f32[8,256]{1,0:T(8,128)S(1)} %copy-done.55, ...), kind=kOutput, calls=%fused_computation.43 | convolution fusion | flops 74973184 | bytes 2056192 | tf_op jit(solution)/shard_map/hts,shp->thp/dot_general | solution.py:128
  79.5 4.1 %fusion.12 = f32[256,40,64]{0,2,1:T(8,128)} fusion(f32[256,40,64]{0,2,1:T(8,128)} %fusion.13, bf16[256,8,64]{0,2,1:T(8,128)(2,1)S(1)} %bitcast.187, f32[8,256]{1,0:T(8,128)S(1)} %copy-done.41, f32[8,256]{1,0:T(8,128)S(1)} %copy-done.50, f32[8,256]{1,0:T(8,128)S(1)} %copy-done.51, f32[8,256]{1,0:T(8,128)S(1)} %copy-done.43, f32[8,256]{1,0:T(8,128)S(1)} %copy-done.44, ...), kind=kOutput, calls=%fused_computation.41 | convolution fusion | flops 74973184 | bytes 2056192 | tf_op jit(solution)/shard_map/hts,shp->thp/dot_general | solution.py:128
  83.6 0.9 copy.43
  84.5 48.6 %collective-permute-done.6 = f32[2560]{0:T(1024)S(1)} collective-permute-done((f32[2560]{0:T(1024)S(1)}, f32[2560]{0:T(1024)S(1)}, u32[]{:S(2)}, u32[]{:S(2)}) %collective-permute-start.6) | collective-permute-done | bytes 10272 | tf_op jit(solution)/shard_map/ppermute | solution.py:18
  133.0 4.3 %collective-permute-start.8 = (f32[2560]{0:T(1024)S(1)}, f32[2560]{0:T(1024)S(1)}, u32[]{:S(2)}, u32[]{:S(2)}) collective-permute-start(f32[2560]{0:T(1024)S(1)} %mul.458), channel_id=1, source_target_pairs={{0,32},{4,36},{8,40},{12,44},{16,48},{20,52},{24,56},{28,60},{32,0... | collective-permute-start | bytes 30728 | tf_op jit(solution)/shard_map/ppermute | solution.py:18
  137.3 5.2 %fusion.11 = f32[256,40,64]{0,2,1:T(8,128)} fusion(f32[256,40,64]{0,2,1:T(8,128)} %fusion.12, bf16[256,8,64]{0,2,1:T(8,128)(2,1)} %bitcast.189, f32[8,256]{1,0:T(8,128)} %get-tuple-element.71, f32[8,256]{1,0:T(8,128)} %get-tuple-element.31, f32[8,256]{1,0:T(8,128)} %get-tuple-element.32, f32[8,256]{1,0:T(8,128)} %get-tuple-element.33, ...), kind=kOutput, calls=%fused_computation.39 | convolution fusion | flops 74973184 | bytes 2056192 | tf_op jit(solution)/shard_map/hts,shp->thp/dot_general | solution.py:128
  142.5 0.1 copy.44
  142.9 1.6 collective-permute-start.10
  144.4 3.0 %add_select_fusion.2 = f32[128,2560]{1,0:T(8,128)} fusion(f32[128,2560]{1,0:T(8,128)} %collective-permute-done.5, f32[128,2560]{1,0:T(8,128)} %add_select_fusion.3, f32[2560]{0:T(1024)S(1)} %collective-permute-done.6, f32[2560]{0:T(1024)S(1)} %mul.450, pred[]{:T(512)S(6)} %eq.277), kind=kLoop, calls=%fused_computation.30 | loop fusion | flops 1638400 | bytes 3952641 | tf_op jit(solution)/shard_map/jit(_where)/select_n | solution.py:141
  147.4 2.0 collective-permute-start.7
  149.6 4.1 %fusion.10 = f32[256,40,64]{0,2,1:T(8,128)} fusion(f32[256,40,64]{0,2,1:T(8,128)} %fusion.11, bf16[256,8,64]{0,2,1:T(8,128)(2,1)S(1)} %bitcast.186, f32[8,256]{1,0:T(8,128)S(1)} %copy-done.31, f32[8,256]{1,0:T(8,128)S(1)} %copy-done.32, f32[8,256]{1,0:T(8,128)S(1)} %copy-done.34, f32[8,256]{1,0:T(8,128)S(1)} %copy-done.35, f32[8,256]{1,0:T(8,128)S(1)} %copy-done.36, ...), kind=kOutput, calls=%fused_computation.37 | convolution fusion | flops 74973184 | bytes 2056192 | tf_op jit(solution)/shard_map/hts,shp->thp/dot_general | solution.py:128
  153.7 3.2 %copy.48 = f32[256,2560]{1,0:T(8,128)} copy(f32[256,2560]{0,1:T(8,128)} %bitcast.62) | data formatting | bytes 5242880 | tf_op jit(solution)/shard_map/concatenate | solution.py:130
  157.0 51.0 %collective-permute-done.7 = f32[128,2560]{1,0:T(8,128)} collective-permute-done((f32[128,2560]{1,0:T(8,128)}, f32[128,2560]{1,0:T(8,128)}, u32[]{:S(2)}, u32[]{:S(2)}) %collective-permute-start.7) | collective-permute-done | bytes 1310752 | tf_op jit(solution)/shard_map/ppermute | solution.py:18
  208.0 1.9 add_select_fusion.1
  209.9 0.6 collective-permute-start.9
  210.5 1.4 fusion.139
  212.0 1.4 fusion.141
  213.4 26.7 %collective-permute-done.9 = f32[128,2560]{1,0:T(8,128)S(1)} collective-permute-done((f32[128,2560]{1,0:T(8,128)S(1)}, f32[128,2560]{1,0:T(8,128)S(1)}, u32[]{:S(2)}, u32[]{:S(2)}) %collective-permute-start.9) | collective-permute-done | bytes 1310752 | tf_op jit(solution)/shard_map/ppermute | solution.py:18
  240.1 0.3 add_select_fusion
  240.4 3.1 %collective-permute-start.11 = (f32[128,2560]{1,0:T(8,128)S(1)}, f32[128,2560]{1,0:T(8,128)S(1)}, u32[]{:S(2)}, u32[]{:S(2)}) collective-permute-start(f32[128,2560]{1,0:T(8,128)S(1)} %add_select_fusion), channel_id=1, source_target_pairs={{0,128},{4,132},{8,136},{12,140},{16,144},{20,148},{24,152},{28,15... | collective-permute-start | bytes 3932168 | tf_op jit(solution)/shard_map/ppermute | solution.py:18
  243.5 1.4 fusion.143
  245.0 26.4 %collective-permute-done.11 = f32[128,2560]{1,0:T(8,128)S(1)} collective-permute-done((f32[128,2560]{1,0:T(8,128)S(1)}, f32[128,2560]{1,0:T(8,128)S(1)}, u32[]{:S(2)}, u32[]{:S(2)}) %collective-permute-start.11) | collective-permute-done | bytes 1310752 | tf_op jit(solution)/shard_map/ppermute | solution.py:18
  271.5 0.1 fusion.147
  271.6 8.4 %multiply_reduce_fusion = f32[256,2560]{1,0:T(8,128)S(1)} fusion(f32[256,6,2560]{2,0,1:T(8,128)} %copy.47, bf16[6,128,2560]{2,1,0:T(8,128)(2,1)S(1)} %fusion.147, bf16[256,2816]{1,0:T(8,128)(2,1)S(1)} %multiply_convert_fusion), kind=kOutput, calls=%fused_computation | convolution fusion | flops 1013841920 | bytes 22347776 | tf_op jit(solution)/shard_map/tn,lnw->tlw/dot_general | solution.py:150
  280.0 1.5 multiply_reduce_fusion.1
  281.6 1.3 multiply_convert_fusion.1
  (160 shorter events, 1.4 us)
Async XLA Ops:
  0.0 5.4 %copy-start = (f32[40,256]{1,0:T(8,128)S(1)}, f32[40,256]{1,0:T(8,128)}, u32[]{:S(2)}) copy-start(f32[40,256]{1,0:T(8,128)} %param.13) | copy-start | bytes 122884
  0.8 13.3 %collective-permute-start = (bf16[3,2816]{1,0:T(4,128)(2,1)S(1)}, bf16[3,2816]{1,0:T(4,128)(2,1)S(1)}, u32[]{:S(2)}, u32[]{:S(2)}) collective-permute-start(bf16[3,2816]{1,0:T(4,128)(2,1)S(1)} %slice.245), channel_id=1, source_target_pairs={{0,4},{4,8},{8,12},{12,16},{16,20},{20,24},{24,28},{28,32},{32,36}... | collective-permute-start | bytes 50696 | tf_op jit(solution)/shard_map/ppermute | solution.py:12
  7.3 18.7 %collective-permute-start.2 = (f32[2560]{0:T(1024)S(1)}, f32[2560]{0:T(1024)S(1)}, u32[]{:S(2)}, u32[]{:S(2)}) collective-permute-start(f32[2560]{0:T(1024)S(1)} %mul.435), channel_id=1, source_target_pairs={{0,4},{4,0},{8,12},{12,8},{16,20},{20,16},{24,28},{28,24},{32,36},... | collective-permute-start | bytes 30728 | tf_op jit(solution)/shard_map/ppermute | solution.py:18
  14.1 6.0 %copy-start.2 = (f32[256,2560]{1,0:T(8,128)S(1)}, f32[256,2560]{1,0:T(8,128)}, u32[]{:S(2)}) copy-start(f32[256,2560]{1,0:T(8,128)} %copy.46) | copy-start | bytes 7864324
  21.7 4.2 %collective-permute-start.1 = (f32[128,2560]{1,0:T(8,128)}, f32[128,2560]{1,0:T(8,128)S(1)}, u32[]{:S(2)}, u32[]{:S(2)}) collective-permute-start(f32[128,2560]{1,0:T(8,128)} %fusion.8), channel_id=1, source_target_pairs={{0,4},{4,0},{8,12},{12,8},{16,20},{20,16},{24,28},{28,24},{32,36},... | collective-permute-start | bytes 3932168 | tf_op jit(solution)/shard_map/ppermute | solution.py:18
  25.9 5.4 %copy-start.61 = (f32[40]{0:T(128)S(1)}, f32[40]{0:T(128)}, u32[]{:S(2)}) copy-start(f32[40]{0:T(128)} %param.15) | copy-start | bytes 484
  28.6 38.9 %collective-permute-start.3 = (f32[128,2560]{1,0:T(8,128)}, f32[128,2560]{1,0:T(8,128)}, u32[]{:S(2)}, u32[]{:S(2)}) collective-permute-start(f32[128,2560]{1,0:T(8,128)} %add_select_fusion.4), channel_id=1, source_target_pairs={{0,8},{4,12},{8,0},{12,4},{16,24},{20,28},{24,16},{28,20},{32,40},... | collective-permute-start | bytes 3932168 | tf_op jit(solution)/shard_map/ppermute | solution.py:18
  55.5 12.1 %collective-permute-start.4 = (f32[2560]{0:T(1024)S(1)}, f32[2560]{0:T(1024)S(1)}, u32[]{:S(2)}, u32[]{:S(2)}) collective-permute-start(f32[2560]{0:T(1024)S(1)} %mul.442), channel_id=1, source_target_pairs={{0,8},{4,12},{8,0},{12,4},{16,24},{20,28},{24,16},{28,20},{32,40},... | collective-permute-start | bytes 30728 | tf_op jit(solution)/shard_map/ppermute | solution.py:18
  58.5 5.3 %copy-start.8 = (f32[256,256]{1,0:T(8,128)}, f32[256,256]{1,0:T(8,128)S(1)}, u32[]{:S(2)}) copy-start(f32[256,256]{1,0:T(8,128)S(1)} %fusion.159) | copy-start | bytes 786436
  67.4 7.6 %copy-start.6 = (f32[256,256]{1,0:T(8,128)S(1)}, f32[256,256]{1,0:T(8,128)}, u32[]{:S(2)}) copy-start(f32[256,256]{1,0:T(8,128)} %get-tuple-element.80) | copy-start | bytes 786436
  67.4 7.6 %copy-start.9 = (f32[256,256]{1,0:T(8,128)S(1)}, f32[256,256]{1,0:T(8,128)}, u32[]{:S(2)}) copy-start(f32[256,256]{1,0:T(8,128)} %copy-done.8) | copy-start | bytes 786436
  67.4 7.6 %copy-start.12 = (bf16[256,512]{0,1:T(8,128)(2,1)S(1)}, bf16[256,512]{0,1:T(8,128)(2,1)}, u32[]{:S(2)}) copy-start(bf16[256,512]{0,1:T(8,128)(2,1)} %copy.41) | copy-start | bytes 786436
  67.4 7.6 %copy-start.13 = (pred[256,256]{1,0:T(8,128)(4,1)S(1)}, pred[256,256]{1,0:T(8,128)(4,1)}, u32[]{:S(2)}) copy-start(pred[256,256]{1,0:T(8,128)(4,1)} %get-tuple-element.85) | copy-start | bytes 196612
  67.4 7.6 %copy-start.15 = (pred[256,256]{1,0:T(8,128)(4,1)S(1)}, pred[256,256]{1,0:T(8,128)(4,1)}, u32[]{:S(2)}) copy-start(pred[256,256]{1,0:T(8,128)(4,1)} %get-tuple-element.88) | copy-start | bytes 196612
  67.4 7.6 %copy-start.17 = (pred[256,256]{1,0:T(8,128)(4,1)S(1)}, pred[256,256]{1,0:T(8,128)(4,1)}, u32[]{:S(2)}) copy-start(pred[256,256]{1,0:T(8,128)(4,1)} %get-tuple-element.89) | copy-start | bytes 196612
  67.4 7.6 %copy-start.19 = (pred[256,256]{1,0:T(8,128)(4,1)S(1)}, pred[256,256]{1,0:T(8,128)(4,1)}, u32[]{:S(2)}) copy-start(pred[256,256]{1,0:T(8,128)(4,1)} %get-tuple-element.86) | copy-start | bytes 196612
  67.4 7.6 %copy-start.21 = (pred[256,256]{1,0:T(8,128)(4,1)S(1)}, pred[256,256]{1,0:T(8,128)(4,1)}, u32[]{:S(2)}) copy-start(pred[256,256]{1,0:T(8,128)(4,1)} %get-tuple-element.87) | copy-start | bytes 196612
  67.4 7.6 %copy-start.23 = (pred[256,256]{1,0:T(8,128)(4,1)S(1)}, pred[256,256]{1,0:T(8,128)(4,1)}, u32[]{:S(2)}) copy-start(pred[256,256]{1,0:T(8,128)(4,1)} %get-tuple-element.79) | copy-start | bytes 196612
  67.5 7.6 %copy-start.25 = (pred[256,256]{1,0:T(8,128)(4,1)S(1)}, pred[256,256]{1,0:T(8,128)(4,1)}, u32[]{:S(2)}) copy-start(pred[256,256]{1,0:T(8,128)(4,1)} %get-tuple-element.83) | copy-start | bytes 196612
  67.5 7.6 %copy-start.42 = (f32[8,256]{1,0:T(8,128)S(1)}, f32[8,256]{1,0:T(8,128)}, u32[]{:S(2)}) copy-start(f32[8,256]{1,0:T(8,128)} %get-tuple-element.73) | copy-start | bytes 24580
  67.5 7.6 %copy-start.52 = (f32[8,256]{1,0:T(8,128)S(1)}, f32[8,256]{1,0:T(8,128)}, u32[]{:S(2)}) copy-start(f32[8,256]{1,0:T(8,128)} %get-tuple-element.50) | copy-start | bytes 24580
  67.5 7.6 %copy-start.53 = (f32[8,256]{1,0:T(8,128)S(1)}, f32[8,256]{1,0:T(8,128)}, u32[]{:S(2)}) copy-start(f32[8,256]{1,0:T(8,128)} %get-tuple-element.51) | copy-start | bytes 24580
  67.5 7.6 %copy-start.54 = (f32[8,256]{1,0:T(8,128)S(1)}, f32[8,256]{1,0:T(8,128)}, u32[]{:S(2)}) copy-start(f32[8,256]{1,0:T(8,128)} %get-tuple-element.52) | copy-start | bytes 24580
  67.5 7.6 %copy-start.55 = (f32[8,256]{1,0:T(8,128)S(1)}, f32[8,256]{1,0:T(8,128)}, u32[]{:S(2)}) copy-start(f32[8,256]{1,0:T(8,128)} %get-tuple-element.53) | copy-start | bytes 24580
  67.5 7.6 %copy-start.56 = (f32[8,256]{1,0:T(8,128)S(1)}, f32[8,256]{1,0:T(8,128)}, u32[]{:S(2)}) copy-start(f32[8,256]{1,0:T(8,128)} %get-tuple-element.54) | copy-start | bytes 24580
  67.5 7.6 %copy-start.57 = (f32[8,256]{1,0:T(8,128)S(1)}, f32[8,256]{1,0:T(8,128)}, u32[]{:S(2)}) copy-start(f32[8,256]{1,0:T(8,128)} %get-tuple-element.55) | copy-start | bytes 24580
  67.5 7.6 %copy-start.58 = (f32[8,256]{1,0:T(8,128)S(1)}, f32[8,256]{1,0:T(8,128)}, u32[]{:S(2)}) copy-start(f32[8,256]{1,0:T(8,128)} %get-tuple-element.56) | copy-start | bytes 24580
  67.5 7.6 %copy-start.59 = (f32[8,256]{1,0:T(8,128)S(1)}, f32[8,256]{1,0:T(8,128)}, u32[]{:S(2)}) copy-start(f32[8,256]{1,0:T(8,128)} %get-tuple-element.57) | copy-start | bytes 24580
  67.6 7.6 %copy-start.60 = (f32[8,256]{1,0:T(8,128)S(1)}, f32[8,256]{1,0:T(8,128)}, u32[]{:S(2)}) copy-start(f32[8,256]{1,0:T(8,128)} %get-tuple-element.58) | copy-start | bytes 24580
  70.7 73.8 %collective-permute-start.5 = (f32[128,2560]{1,0:T(8,128)}, f32[128,2560]{1,0:T(8,128)}, u32[]{:S(2)}, u32[]{:S(2)}) collective-permute-start(f32[128,2560]{1,0:T(8,128)} %add_select_fusion.3), channel_id=1, source_target_pairs={{0,16},{4,20},{8,24},{12,28},{16,0},{20,4},{24,8},{28,12},{32,48},... | collective-permute-start | bytes 3932168 | tf_op jit(solution)/shard_map/ppermute | solution.py:18
  75.2 4.2 %copy-start.11 = (bf16[256,512]{0,1:T(8,128)(2,1)S(1)}, bf16[256,512]{0,1:T(8,128)(2,1)}, u32[]{:S(2)}) copy-start(bf16[256,512]{0,1:T(8,128)(2,1)} %copy.42) | copy-start | bytes 786436
  75.2 4.2 %copy-start.41 = (f32[8,256]{1,0:T(8,128)S(1)}, f32[8,256]{1,0:T(8,128)}, u32[]{:S(2)}) copy-start(f32[8,256]{1,0:T(8,128)} %get-tuple-element.72) | copy-start | bytes 24580
  75.2 4.2 %copy-start.43 = (f32[8,256]{1,0:T(8,128)S(1)}, f32[8,256]{1,0:T(8,128)}, u32[]{:S(2)}) copy-start(f32[8,256]{1,0:T(8,128)} %get-tuple-element.43) | copy-start | bytes 24580
  75.2 4.2 %copy-start.44 = (f32[8,256]{1,0:T(8,128)S(1)}, f32[8,256]{1,0:T(8,128)}, u32[]{:S(2)}) copy-start(f32[8,256]{1,0:T(8,128)} %get-tuple-element.44) | copy-start | bytes 24580
  75.2 4.2 %copy-start.45 = (f32[8,256]{1,0:T(8,128)S(1)}, f32[8,256]{1,0:T(8,128)}, u32[]{:S(2)}) copy-start(f32[8,256]{1,0:T(8,128)} %get-tuple-element.45) | copy-start | bytes 24580
  75.3 4.2 %copy-start.46 = (f32[8,256]{1,0:T(8,128)S(1)}, f32[8,256]{1,0:T(8,128)}, u32[]{:S(2)}) copy-start(f32[8,256]{1,0:T(8,128)} %get-tuple-element.46) | copy-start | bytes 24580
  79.4 53.6 %collective-permute-start.6 = (f32[2560]{0:T(1024)S(1)}, f32[2560]{0:T(1024)S(1)}, u32[]{:S(2)}, u32[]{:S(2)}) collective-permute-start(f32[2560]{0:T(1024)S(1)} %mul.450), channel_id=1, source_target_pairs={{0,16},{4,20},{8,24},{12,28},{16,0},{20,4},{24,8},{28,12},{32,48},... | collective-permute-start | bytes 30728 | tf_op jit(solution)/shard_map/ppermute | solution.py:18
  133.0 9.8 %collective-permute-start.8 = (f32[2560]{0:T(1024)S(1)}, f32[2560]{0:T(1024)S(1)}, u32[]{:S(2)}, u32[]{:S(2)}) collective-permute-start(f32[2560]{0:T(1024)S(1)} %mul.458), channel_id=1, source_target_pairs={{0,32},{4,36},{8,40},{12,44},{16,48},{20,52},{24,56},{28,60},{32,0... | collective-permute-start | bytes 30728 | tf_op jit(solution)/shard_map/ppermute | solution.py:18
  142.7 6.7 %copy-start.7 = (f32[256,256]{1,0:T(8,128)S(1)}, f32[256,256]{1,0:T(8,128)}, u32[]{:S(2)}) copy-start(f32[256,256]{1,0:T(8,128)} %get-tuple-element.80) | copy-start | bytes 786436
  142.7 6.7 %copy-start.10 = (f32[256,256]{1,0:T(8,128)S(1)}, f32[256,256]{1,0:T(8,128)}, u32[]{:S(2)}) copy-start(f32[256,256]{1,0:T(8,128)} %copy-done.8) | copy-start | bytes 786436
  142.7 6.7 %copy-start.14 = (pred[256,256]{1,0:T(8,128)(4,1)S(1)}, pred[256,256]{1,0:T(8,128)(4,1)}, u32[]{:S(2)}) copy-start(pred[256,256]{1,0:T(8,128)(4,1)} %get-tuple-element.85) | copy-start | bytes 196612
  142.7 6.7 %copy-start.16 = (pred[256,256]{1,0:T(8,128)(4,1)S(1)}, pred[256,256]{1,0:T(8,128)(4,1)}, u32[]{:S(2)}) copy-start(pred[256,256]{1,0:T(8,128)(4,1)} %get-tuple-element.88) | copy-start | bytes 196612
  142.7 6.7 %copy-start.18 = (pred[256,256]{1,0:T(8,128)(4,1)S(1)}, pred[256,256]{1,0:T(8,128)(4,1)}, u32[]{:S(2)}) copy-start(pred[256,256]{1,0:T(8,128)(4,1)} %get-tuple-element.89) | copy-start | bytes 196612
  142.7 6.7 %copy-start.20 = (pred[256,256]{1,0:T(8,128)(4,1)S(1)}, pred[256,256]{1,0:T(8,128)(4,1)}, u32[]{:S(2)}) copy-start(pred[256,256]{1,0:T(8,128)(4,1)} %get-tuple-element.86) | copy-start | bytes 196612
  142.7 6.7 %copy-start.22 = (pred[256,256]{1,0:T(8,128)(4,1)S(1)}, pred[256,256]{1,0:T(8,128)(4,1)}, u32[]{:S(2)}) copy-start(pred[256,256]{1,0:T(8,128)(4,1)} %get-tuple-element.87) | copy-start | bytes 196612
  142.7 6.7 %copy-start.24 = (pred[256,256]{1,0:T(8,128)(4,1)S(1)}, pred[256,256]{1,0:T(8,128)(4,1)}, u32[]{:S(2)}) copy-start(pred[256,256]{1,0:T(8,128)(4,1)} %get-tuple-element.79) | copy-start | bytes 196612
  142.7 6.7 %copy-start.26 = (pred[256,256]{1,0:T(8,128)(4,1)S(1)}, pred[256,256]{1,0:T(8,128)(4,1)}, u32[]{:S(2)}) copy-start(pred[256,256]{1,0:T(8,128)(4,1)} %get-tuple-element.83) | copy-start | bytes 196612
  142.8 6.7 %copy-start.31 = (f32[8,256]{1,0:T(8,128)S(1)}, f32[8,256]{1,0:T(8,128)}, u32[]{:S(2)}) copy-start(f32[8,256]{1,0:T(8,128)} %get-tuple-element.70) | copy-start | bytes 24580
  142.8 6.7 %copy-start.32 = (f32[8,256]{1,0:T(8,128)S(1)}, f32[8,256]{1,0:T(8,128)}, u32[]{:S(2)}) copy-start(f32[8,256]{1,0:T(8,128)} %get-tuple-element.42) | copy-start | bytes 24580
  142.8 6.7 %copy-start.33 = (f32[8,256]{1,0:T(8,128)S(1)}, f32[8,256]{1,0:T(8,128)}, u32[]{:S(2)}) copy-start(f32[8,256]{1,0:T(8,128)} %get-tuple-element.23) | copy-start | bytes 24580
  142.8 6.7 %copy-start.34 = (f32[8,256]{1,0:T(8,128)S(1)}, f32[8,256]{1,0:T(8,128)}, u32[]{:S(2)}) copy-start(f32[8,256]{1,0:T(8,128)} %get-tuple-element.24) | copy-start | bytes 24580
  142.8 6.7 %copy-start.35 = (f32[8,256]{1,0:T(8,128)S(1)}, f32[8,256]{1,0:T(8,128)}, u32[]{:S(2)}) copy-start(f32[8,256]{1,0:T(8,128)} %get-tuple-element.25) | copy-start | bytes 24580
  142.8 6.7 %copy-start.36 = (f32[8,256]{1,0:T(8,128)S(1)}, f32[8,256]{1,0:T(8,128)}, u32[]{:S(2)}) copy-start(f32[8,256]{1,0:T(8,128)} %get-tuple-element.26) | copy-start | bytes 24580
  142.8 6.7 %copy-start.37 = (f32[8,256]{1,0:T(8,128)S(1)}, f32[8,256]{1,0:T(8,128)}, u32[]{:S(2)}) copy-start(f32[8,256]{1,0:T(8,128)} %get-tuple-element.27) | copy-start | bytes 24580
  142.8 6.7 %copy-start.38 = (f32[8,256]{1,0:T(8,128)S(1)}, f32[8,256]{1,0:T(8,128)}, u32[]{:S(2)}) copy-start(f32[8,256]{1,0:T(8,128)} %get-tuple-element.28) | copy-start | bytes 24580
  142.8 6.7 %copy-start.39 = (f32[8,256]{1,0:T(8,128)S(1)}, f32[8,256]{1,0:T(8,128)}, u32[]{:S(2)}) copy-start(f32[8,256]{1,0:T(8,128)} %get-tuple-element.29) | copy-start | bytes 24580
  142.8 6.7 %copy-start.40 = (f32[8,256]{1,0:T(8,128)S(1)}, f32[8,256]{1,0:T(8,128)}, u32[]{:S(2)}) copy-start(f32[8,256]{1,0:T(8,128)} %get-tuple-element.30) | copy-start | bytes 24580
  142.9 14.0 %collective-permute-start.10 = (f32[2560]{0:T(1024)S(1)}, f32[2560]{0:T(1024)S(1)}, u32[]{:S(2)}, u32[]{:S(2)}) collective-permute-start(f32[2560]{0:T(1024)S(1)} %mul.466), channel_id=1, source_target_pairs={{0,64},{4,68},{8,72},{12,76},{16,80},{20,84},{24,88},{28,92},{32,9... | collective-permute-start | bytes 30728 | tf_op jit(solution)/shard_map/ppermute | solution.py:18
  147.4 60.5 %collective-permute-start.7 = (f32[128,2560]{1,0:T(8,128)}, f32[128,2560]{1,0:T(8,128)}, u32[]{:S(2)}, u32[]{:S(2)}) collective-permute-start(f32[128,2560]{1,0:T(8,128)} %add_select_fusion.2), channel_id=1, source_target_pairs={{0,32},{4,36},{8,40},{12,44},{16,48},{20,52},{24,56},{28,60},{32,0... | collective-permute-start | bytes 3932168 | tf_op jit(solution)/shard_map/ppermute | solution.py:18
  209.9 30.2 %collective-permute-start.9 = (f32[128,2560]{1,0:T(8,128)S(1)}, f32[128,2560]{1,0:T(8,128)S(1)}, u32[]{:S(2)}, u32[]{:S(2)}) collective-permute-start(f32[128,2560]{1,0:T(8,128)S(1)} %add_select_fusion.1), channel_id=1, source_target_pairs={{0,64},{4,68},{8,72},{12,76},{16,80},{20,84},{24,88},{28,92},{32,9... | collective-permute-start | bytes 3932168 | tf_op jit(solution)/shard_map/ppermute | solution.py:18
  240.4 31.1 %collective-permute-start.11 = (f32[128,2560]{1,0:T(8,128)S(1)}, f32[128,2560]{1,0:T(8,128)S(1)}, u32[]{:S(2)}, u32[]{:S(2)}) collective-permute-start(f32[128,2560]{1,0:T(8,128)S(1)} %add_select_fusion), channel_id=1, source_target_pairs={{0,128},{4,132},{8,136},{12,140},{16,144},{20,148},{24,152},{28,15... | collective-permute-start | bytes 3932168 | tf_op jit(solution)/shard_map/ppermute | solution.py:18
  271.6 8.4 %copy-start.3 = (f32[256,2560]{1,0:T(8,128)S(1)}, f32[256,2560]{1,0:T(8,128)}, u32[]{:S(2)}) copy-start(f32[256,2560]{1,0:T(8,128)} %copy.48) | copy-start | bytes 7864324
  271.6 8.4 %copy-start.4 = (bf16[256,2560]{1,0:T(8,128)(2,1)S(1)}, bf16[256,2560]{1,0:T(8,128)(2,1)}, u32[]{:S(2)}) copy-start(bf16[256,2560]{1,0:T(8,128)(2,1)} %param.12) | copy-start | bytes 3932164
  271.6 8.4 %copy-start.27 = (f32[2560]{0:T(1024)S(1)}, f32[2560]{0:T(1024)}, u32[]{:S(2)}) copy-start(f32[2560]{0:T(1024)} %mul.482) | copy-start | bytes 30724
  (10 other events, 34.5 us)
where the time goes:
time: 284 us; the launch traced here: 283 us
  waiting for transfers between devices  153 us (54%)
  local copies, waits for them, and re-layouts  41.8 us (15%)
  matrix products  32.9 us (12%)
  other arithmetic  31.2 us (11%)
  starting transfers between devices  21.9 us (8%)
    ppermute x11, waiting for transfers between devices, partner(): return lax.ppermute(value, axis, pairs)  153 us
    dot_general x5, matrix products, per_device(): jnp.einsum('hts,shp->thp', mixing, values, preferred_element_type=jnp.flo...  22.8 us
    mul x2, local copies, waits for them, and re-layouts, per_device(): shaped * jnp.transpose(factor, (2, 1, 0))[:, :, :, None]  22.4 us
    ppermute x11, starting transfers between devices, partner(): return lax.ppermute(value, axis, pairs)  20.2 us
    select_n x5, other arithmetic, per_device(): jnp.where(on_top, far_state * block_total[None, :] + running, running * f...  11 us
    dot_general x1, matrix products, per_device(): jnp.einsum('tn,lnw->tlw', queries, stacked, preferred_element_type=jnp.fl...  8.38 us
    another operation x6, other arithmetic  7.61 us
    slice x6, local copies, waits for them, and re-layouts, per_device(): xs[:, block_start * head_dim:(block_start + per_block) * head_dim]  7.29 us
  transfers between devices with their start and end apart: 12, of which 4 were waited for; matrix products, arithmetic and copies ran while one was open for 30% of the time, Pallas kernels for 0%

commit v1 on v0

v1 whole, which is shorter than its diff:
```python
import jax
import jax.numpy as jnp
from jax import lax
from jax.experimental import pallas as pl
from jax.experimental.pallas import tpu as pltpu
from jax.sharding import PartitionSpec as P

EPS = 1e-05
F32 = jnp.float32
BF16 = jnp.bfloat16
MESH = pl.DeviceIdType.MESH

TOK = 256
WIDTH = 2560
HEADS = 40
HD = 64
STATE = 128
CH = 2816
TAPS = 4
NX, NZ = 4, 8
HALF = WIDTH // 2
HALO = 16
CR = 128
NC = HALF // CR
HPC = CR // HD
XR = CR + 16
BR = 256
NB = WIDTH // BR
HPB = BR // HD

L1, L2, L3, TT, X4, X5 = range(6)


def kernel(
    mixed,
    gate,
    ld,
    lam,
    cw,
    cb,
    ng,
    skip,
    segl,
    out,
    halo,
    pad,
    xst,
    keys,
    quer,
    ef,
    sibe,
    cacc,
    snd,
    lbuf,
    tbuf,
    dec,
    dsrc,
    theta,
    pbuf,
    cum,
    cumt,
    endw,
    entry,
    sct,
    lev,
    acc,
    gt,
    halo_s,
    halo_r,
    th_s,
    th_r,
    e_s,
    e_r,
    rsem,
    ssem,
    ssem2,
    sib_s,
    sib_r,
):
    g = lax.axis_index("group")
    core = lax.rem(g, 2)
    z = lax.rem(g // 2, NZ)
    x = g // (2 * NZ)
    ngroups = 2 * NZ * NX

    def at(xx, zz, cc):
        return (xx * NZ + zz) * 2 + cc

    sib = at(x, z, 1 - core)
    zup = at(x, lax.rem(z + 1, NZ), core)
    zdn = at(x, lax.rem(z + NZ - 1, NZ), core)
    zup3 = at(x, lax.rem(z + 3, NZ), core)
    zdn3 = at(x, lax.rem(z + NZ - 3, NZ), core)
    xup = at(lax.rem(x + 1, NX), z, core)
    xdn = at(lax.rem(x + NX - 1, NX), z, core)
    gnext = lax.rem(g + 1, ngroups)
    gprev = lax.rem(g + ngroups - 1, ngroups)

    barrier = pltpu.get_barrier_semaphore()
    partners = (sib, zup, zdn, zup3, zdn3, xup, xdn, gnext, gprev)
    for peer in partners:
        pl.semaphore_signal(barrier, inc=1, device_id={"group": peer}, device_id_type=MESH)

    def rcopy(src, dst, ss, rs, peer):
        return pltpu.make_async_remote_copy(
            src_ref=src,
            dst_ref=dst,
            send_sem=ss,
            recv_sem=rs,
            device_id={"group": peer},
            device_id_type=MESH,
        )

    first = g * TOK
    b1 = segl[0]
    b2 = segl[0] + segl[1]

    def seg_of(pos):
        s = (pos >= b1).astype(jnp.int32) + (pos >= b2).astype(jnp.int32)
        return jnp.where(pos >= 0, s, -1)

    lane_pos = first + lax.broadcasted_iota(jnp.int32, (8, TOK), 1)[0:1]
    seg_row = seg_of(lane_pos)
    last_row = seg_of(jnp.full((1, TOK), first + TOK - 1, jnp.int32))
    prev_row = seg_of(jnp.full((1, TOK), first - 1, jnp.int32))

    c = ld[...]
    lane = lax.broadcasted_iota(jnp.int32, (HEADS, TOK), 1)
    step = 1
    while step < TOK:
        c = c + jnp.where(lane >= step, pltpu.roll(c, step, 1), 0.0)
        step *= 2
    cum[...] = c
    c_end = c[:, TOK - 1 : TOK]
    endw[...] = jnp.exp(c_end - c) * (seg_row == last_row).astype(F32)
    entry[...] = jnp.exp(c) * (seg_row == prev_row).astype(F32)
    theta[0] = jnp.broadcast_to(jnp.exp(c_end), (HEADS, 128)) * (last_row == prev_row).astype(F32)[
        :, 0:128
    ]
    cpad = jnp.concatenate([c, jnp.zeros((128 - HEADS, TOK), F32)], axis=0)
    cumt[...] = jnp.concatenate([cpad[:, 0:128].T, cpad[:, 128:256].T], axis=0)

    si = lax.broadcasted_iota(jnp.int32, (128, 128), 0)
    ti = lax.broadcasted_iota(jnp.int32, (128, 128), 1)
    diff = si ^ ti
    lv = jnp.zeros((128, 128), jnp.int32)
    for b in range(7):
        lv = lv + (diff >= 2**b).astype(jnp.int32)
    lev[...] = lv

    pl.semaphore_wait(barrier, len(partners))

    halo_copy = rcopy(mixed.at[pl.ds(TOK - HALO, HALO)], halo, halo_s, halo_r, gnext)
    halo_copy.start()
    th_copy = rcopy(theta.at[0], theta.at[1], th_s, th_r, sib)
    th_copy.start()

    col_pos = first + lax.broadcasted_iota(jnp.int32, (TOK, 256), 0)
    seg_col = seg_of(col_pos)
    same = [None] + [seg_of(col_pos - t) == seg_col for t in range(1, TAPS)]

    def conv(cols):
        cur = mixed[:, cols].astype(F32)
        pad[8 : 8 + TOK, :] = cur
        pad[0:8, :] = halo[HALO - 8 : HALO, cols].astype(F32)
        total = cb[:, cols] + cw[0:1, cols] * cur
        for t in range(1, TAPS):
            piece = pad[8 - t : 8 - t + TOK, :]
            total = total + cw[t : t + 1, cols] * jnp.where(same[t], piece, 0.0)
        return total * (1.0 / (1.0 + jnp.exp(-total)))

    halo_copy.wait_recv()
    kq = conv(pl.ds(WIDTH, 2 * STATE))
    keys[...] = kq[:, 0:STATE].astype(BF16)
    quer[...] = kq[:, STATE : 2 * STATE].astype(BF16)

    def e_copy(i):
        rows = pl.ds(pl.multiple_of(i * BR, BR), BR)
        return rcopy(ef.at[rows], sibe.at[rows], e_s.at[i], e_r.at[i], sib)

    def conv_step(i, _):
        base = pl.multiple_of(i * BR, BR)
        act = conv(pl.ds(base, BR)).T.astype(BF16)
        xst[pl.ds(base, BR), :] = act
        parts = []
        for j in range(HPB):
            w = endw[pl.ds(i * HPB + j, 1), :]
            parts.append((act[j * HD : (j + 1) * HD].astype(F32) * w).astype(BF16))
        e = jnp.dot(jnp.concatenate(parts, axis=0), keys[...], preferred_element_type=F32)
        ef[pl.ds(base, BR), :] = e
        e_copy(i).start()
        return 0

    lax.fori_loop(0, NB, conv_step, 0)

    th_copy.wait_recv()
    dsrc[0] = theta[0] * theta[1]
    pbuf[0] = jnp.ones((HEADS, 128), F32)

    @pl.when(core == 1)
    def _():
        pbuf[1] = theta[1]

    @pl.when(core == 0)
    def _():
        pbuf[1] = jnp.ones((HEADS, 128), F32)

    half = core * HALF

    def mine(i):
        return pl.ds(pl.multiple_of(half + i * CR, CR), CR)

    def sub(i):
        return pl.ds(pl.multiple_of(i * CR, CR), CR)

    def chunk(i):
        return core * NC + i

    def lcopy(s, i, peer, ss):
        dst = lbuf.at[s, chunk(i)]
        return rcopy(dst, dst, ss.at[s, i], rsem.at[s, i], peer)

    def scopy(k, s, i, peer, ss):
        return rcopy(snd.at[k, i], lbuf.at[s, chunk(i)], ss.at[s, i], rsem.at[s, i], peer)

    def dcopy(src, slot, s, peer, ss):
        return rcopy(src, dec.at[slot], ss.at[s, NC], rsem.at[s, NC], peer)

    def sibcopy(k, s, i):
        dst = lbuf.at[k, chunk(i)]
        return rcopy(dst, dst, sib_s.at[s, i], sib_r.at[s, i], sib)

    def sibwait(k, s, i):
        dst = lbuf.at[k, (1 - core) * NC + i]
        rcopy(dst, dst, sib_s.at[s, i], sib_r.at[s, i], sib).wait_recv()

    def tcopy(i, peer, ss):
        dst = tbuf.at[i]
        return rcopy(dst, dst, ss.at[TT, i], rsem.at[TT, i], peer)

    def x4copy(i):
        return rcopy(
            tbuf.at[i], lbuf.at[3, chunk(i)], ssem.at[X4, i], rsem.at[X4, i], xup
        )

    def encode(v):
        q, ex = [], []
        for j in range(HPC):
            blk = v[j * HD : (j + 1) * HD]
            top = jnp.max(jnp.abs(blk), axis=0, keepdims=True)
            e = jnp.ceil(jnp.log2(jnp.maximum(top, 1e-30))) - 14.0
            q.append(jnp.floor(blk * (1.0 / jnp.exp2(e)) + 0.5))
            ex.append(jnp.broadcast_to(e, (16 // HPC, 128)))
        return jnp.concatenate(q + ex, axis=0).astype(jnp.int32).astype(jnp.int16)

    def decode(ref):
        v = ref[...].astype(jnp.int32).astype(F32)
        parts = []
        for j in range(HPC):
            r = CR + j * (16 // HPC)
            parts.append(v[j * HD : (j + 1) * HD] * jnp.exp2(v[r : r + 1]))
        return jnp.concatenate(parts, axis=0)

    def scaled_add(recv, dref, base, i):
        rows = []
        for j in range(HPC):
            h = core * (HEADS // 2) + i * HPC + j
            d = dref[pl.ds(h, 1), :]
            rows.append(recv[j * HD : (j + 1) * HD] * d + base[j * HD : (j + 1) * HD])
        return jnp.concatenate(rows, axis=0)

    is_even = lax.rem(z, 2) == 0
    z4 = lax.rem(z, 4)

    @pl.when(is_even)
    def _():
        dcopy(dsrc.at[0], 0, L1, zup, ssem).start()

    def wait_e(i, _):
        e_copy(i).wait_recv()
        return 0

    lax.fori_loop(0, NB, wait_e, 0)

    def chip_step(i, _):
        rows = mine(i)
        own = ef[rows, :]
        other = sibe[rows, :]

        @pl.when(core == 1)
        def _():
            cacc[sub(i), :] = scaled_add(other, theta.at[0], own, i)

        @pl.when(core == 0)
        def _():
            cacc[sub(i), :] = scaled_add(own, theta.at[1], other, i)

        @pl.when(is_even)
        def _():
            snd[0, i] = encode(cacc[sub(i), :])
            scopy(0, 0, i, zup, ssem).start()

        return 0

    lax.fori_loop(0, NC, chip_step, 0)

    s_t = lax.dot_general(
        keys[...], quer[...], (((1,), (1,)), ((), ())), preferred_element_type=F32
    )
    rowi = lax.broadcasted_iota(jnp.int32, (TOK, TOK), 0)
    coli = lax.broadcasted_iota(jnp.int32, (TOK, TOK), 1)
    ok = (rowi <= coli) & (seg_col == seg_row)
    sct[...] = jnp.where(ok, s_t, 0.0)

    def local_heads(i):
        rolled = pltpu.roll(cumt[...], lax.rem(128 - i * HPB, 128), 1)
        for j in range(HPB):
            h = i * HPB + j
            rows = pl.ds(pl.multiple_of(h * HD, HD), HD)
            ccol = rolled[:, j : j + 1]
            crow = cum[pl.ds(h, 1), :]

            def lam_row(l, lo):
                return lam[h, l : l + 1, lo : lo + 128]

            def picked(lo):
                p = jnp.broadcast_to(lam_row(7, lo), (128, 128))
                for l in range(7):
                    p = jnp.where(lev[...] == l, lam_row(l, lo), p)
                return p

            def mix(slo, tlo, pick):
                gap = crow[:, tlo : tlo + 128] - ccol[slo : slo + 128]
                decay = jnp.exp(jnp.minimum(gap, 0.0))
                return (sct[slo : slo + 128, tlo : tlo + 128] * pick * decay).astype(BF16)

            m00 = mix(0, 0, picked(0))
            m01 = mix(0, 128, lam_row(8, 128))
            m11 = mix(128, 128, picked(128))
            xs = xst[rows, :]
            left = jnp.dot(xs[:, 0:128], m00, preferred_element_type=F32)
            right = jnp.dot(xs, jnp.concatenate([m01, m11], axis=0), preferred_element_type=F32)
            acc[rows, :] = jnp.concatenate([left, right], axis=1) + skip[h] * xs.astype(F32)

    @pl.when(is_even)
    def _():
        pbuf[2] = pbuf[1]

    @pl.when(jnp.logical_not(is_even))
    def _():
        dcopy(dsrc.at[0], 0, L1, zup, ssem).wait_recv()
        pbuf[2] = pbuf[1] * dec[0]
        dsrc[1] = dec[0] * dsrc[0]

        @pl.when(z4 == 1)
        def _():
            dcopy(dsrc.at[1], 1, L2, zup, ssem).start()

    def l1_step(i, _):
        local_heads(i)

        @pl.when(jnp.logical_not(is_even))
        def _():
            scopy(0, 0, i, zup, ssem).wait_recv()
            sibcopy(0, L1, i).start()
            s = scaled_add(decode(lbuf.at[0, chunk(i)]), dsrc.at[0], cacc[sub(i), :], i)
            cacc[sub(i), :] = s

            @pl.when(z4 == 1)
            def _():
                snd[1, i] = encode(s)
                scopy(1, 1, i, zup, ssem).start()

        return 0

    lax.fori_loop(0, NC, l1_step, 0)

    @pl.when(z4 < 2)
    def _():
        pbuf[3] = pbuf[2]

    @pl.when(z4 >= 2)
    def _():
        dcopy(dec.at[1], 1, L2, zup, ssem).wait_recv()
        pbuf[3] = pbuf[2] * dec[1]

        @pl.when(z4 == 2)
        def _():
            dcopy(dec.at[1], 1, L2, zup, ssem).start()

        @pl.when(z4 == 3)
        def _():
            dsrc[2] = dec[1] * dsrc[1]

            @pl.when(z == 3)
            def _():
                dcopy(dsrc.at[2], 2, L3, zup, ssem).start()
                dcopy(dsrc.at[2], 2, L3, zdn3, ssem2).start()

    def gate_block(i):
        cols = pl.ds(pl.multiple_of(i * BR, BR), BR)
        v = gate[:, cols].astype(F32)
        gt[cols, :] = (v * (1.0 / (1.0 + jnp.exp(-v)))).T

    def l2_step(i, _):
        gate_block(i)

        @pl.when(z4 >= 2)
        def _():
            lcopy(1, i, zup, ssem).wait_recv()

            @pl.when(z4 == 2)
            def _():
                lcopy(1, i, zup, ssem).start()

            sibcopy(1, L2, i).start()

            @pl.when(z4 == 3)
            def _():
                s = scaled_add(decode(lbuf.at[1, chunk(i)]), dsrc.at[1], cacc[sub(i), :], i)
                cacc[sub(i), :] = s

                @pl.when(z == 3)
                def _():
                    snd[2, i] = encode(s)
                    scopy(2, 2, i, zup, ssem).start()
                    scopy(2, 2, i, zdn3, ssem2).start()

        return 0

    lax.fori_loop(0, NC, l2_step, 0)

    l3_in = jnp.logical_or(z >= 4, z == 0)

    def l3_relay(make):
        @pl.when(z == 4)
        def _():
            make(zup)

        @pl.when(jnp.logical_or(z == 0, z == 7))
        def _():
            make(zdn)

    @pl.when(z < 4)
    def _():
        pbuf[4] = pbuf[3]

    @pl.when(l3_in)
    def _():
        dcopy(dec.at[2], 2, L3, zup, ssem).wait_recv()
        l3_relay(lambda peer: dcopy(dec.at[2], 2, L3, peer, ssem).start())

        @pl.when(z >= 4)
        def _():
            pbuf[4] = pbuf[3] * dec[2]

        @pl.when(z == 7)
        def _():
            dec[3] = dec[2] * dsrc[2]

            @pl.when(x < NX - 1)
            def _():
                dcopy(dec.at[3], 3, TT, zup, ssem).start()
                dcopy(dec.at[3], 3, TT, zdn, ssem2).start()

                @pl.when(lax.rem(x, 2) == 0)
                def _():
                    dcopy(dec.at[3], 4, X4, xup, ssem).start()

    def l3_step(i, _):
        @pl.when(l3_in)
        def _():
            lcopy(2, i, zup, ssem).wait_recv()
            l3_relay(lambda peer: lcopy(2, i, peer, ssem).start())

            @pl.when(z >= 4)
            def _():
                sibcopy(2, L3, i).start()

            @pl.when(z == 7)
            def _():
                s = scaled_add(decode(lbuf.at[2, chunk(i)]), dsrc.at[2], cacc[sub(i), :], i)
                tbuf[i] = encode(s)

                @pl.when(x < NX - 1)
                def _():
                    tcopy(i, zup, ssem).start()
                    tcopy(i, zdn, ssem2).start()

                    @pl.when(lax.rem(x, 2) == 0)
                    def _():
                        x4copy(i).start()

        return 0

    lax.fori_loop(0, NC, l3_step, 0)

    t_in = jnp.logical_and(z < 7, x < NX - 1)

    def t_relay(make):
        @pl.when(z <= 2)
        def _():
            make(zup)

        @pl.when(z >= 5)
        def _():
            make(zdn)

    @pl.when(t_in)
    def _():
        dcopy(dec.at[3], 3, TT, zup, ssem).wait_recv()
        t_relay(lambda peer: dcopy(dec.at[3], 3, TT, peer, ssem).start())

        @pl.when(lax.rem(x, 2) == 0)
        def _():
            dcopy(dec.at[3], 4, X4, xup, ssem).start()

    def t_step(i, _):
        @pl.when(t_in)
        def _():
            tcopy(i, zup, ssem).wait_recv()
            t_relay(lambda peer: tcopy(i, peer, ssem).start())

            @pl.when(lax.rem(x, 2) == 0)
            def _():
                x4copy(i).start()

        return 0

    lax.fori_loop(0, NC, t_step, 0)

    def far(level):
        def body(i, _):
            base = pl.multiple_of(i * BR, BR)
            if level == 0:
                state = sibe[pl.ds(base, BR), :].astype(BF16)
            else:
                parts = []
                for m in range(HPB // HPC):
                    v = decode(lbuf.at[level - 1, i * (HPB // HPC) + m])
                    for j in range(HPC):
                        p = pbuf[level, pl.ds(i * HPB + m * HPC + j, 1), :]
                        parts.append((v[j * HD : (j + 1) * HD] * p).astype(BF16))
                state = jnp.concatenate(parts, axis=0)
            read = lax.dot_general(
                state, quer[...], (((1,), (1,)), ((), ())), preferred_element_type=F32
            )
            for j in range(HPB):
                h = i * HPB + j
                coef = lam[h, 9 + level : 10 + level, :] * entry[pl.ds(h, 1), :]
                rows = pl.ds(pl.multiple_of(base + j * HD, HD), HD)
                acc[rows, :] = acc[rows, :] + read[j * HD : (j + 1) * HD] * coef
            return 0

        lax.fori_loop(0, NB, body, 0)

    def sib_wait_all(k, s):
        def body(i, _):
            sibwait(k, s, i)
            return 0

        lax.fori_loop(0, NC, body, 0)

    @pl.when(core == 1)
    def _():
        far(0)

    @pl.when(jnp.logical_not(is_even))
    def _():
        sib_wait_all(0, L1)
        far(1)

    @pl.when(z4 >= 2)
    def _():
        sib_wait_all(1, L2)
        far(2)

    @pl.when(z >= 4)
    def _():
        sib_wait_all(2, L3)
        far(3)

    x_odd = lax.rem(x, 2) == 1

    @pl.when(jnp.logical_not(x_odd))
    def _():
        pbuf[5] = pbuf[4]

    @pl.when(x_odd)
    def _():
        dcopy(dec.at[3], 4, X4, xup, ssem).wait_recv()
        pbuf[5] = pbuf[4] * dec[4]

    def x5copy(i, peer, ss):
        return rcopy(snd.at[3, i], lbuf.at[4, chunk(i)], ss.at[X5, i], rsem.at[X5, i], peer)

    def x5relay(i):
        dst = lbuf.at[4, chunk(i)]
        return rcopy(dst, dst, ssem.at[X5, i], rsem.at[X5, i], xdn)

    def x4_step(i, _):
        @pl.when(x_odd)
        def _():
            x4copy(i).wait_recv()
            sibcopy(3, X4, i).start()

            @pl.when(x == 1)
            def _():
                s = scaled_add(
                    decode(lbuf.at[3, chunk(i)]), dec.at[3], decode(tbuf.at[i]), i
                )
                snd[3, i] = encode(s)
                x5copy(i, xup, ssem).start()
                x5copy(i, xdn, ssem2).start()

        return 0

    lax.fori_loop(0, NC, x4_step, 0)

    def x5_step(i, _):
        @pl.when(x != 1)
        def _():
            x5relay(i).wait_recv()

            @pl.when(x == 0)
            def _():
                x5relay(i).start()

            @pl.when(x >= 2)
            def _():
                sibcopy(4, X5, i).start()

        return 0

    @pl.when(x_odd)
    def _():
        sib_wait_all(3, X4)
        far(4)

    lax.fori_loop(0, NC, x5_step, 0)

    @pl.when(x >= 2)
    def _():
        sib_wait_all(4, X5)
        far(5)

    def gate_step(i, ssq):
        rows = pl.ds(pl.multiple_of(i * BR, BR), BR)
        v = acc[rows, :] * gt[rows, :]
        acc[rows, :] = v
        return ssq + jnp.sum((v * v).reshape(BR // 8, 8, TOK), axis=0)

    ssq = lax.fori_loop(0, NB, gate_step, jnp.zeros((8, TOK), F32))
    scale = lax.rsqrt(jnp.sum(ssq, axis=0, keepdims=True) * (1.0 / WIDTH) + EPS)

    def out_step(i, _):
        cols = pl.ds(pl.multiple_of(i * BR, BR), BR)
        v = (acc[cols, :] * scale).T
        out[:, cols] = (v * ng[:, cols]).astype(BF16)
        return 0

    lax.fori_loop(0, NB, out_step, 0)

    halo_copy.wait_send()
    th_copy.wait_send()

    def e_done(i, _):
        e_copy(i).wait_send()
        return 0

    lax.fori_loop(0, NB, e_done, 0)

    def drain(i, _):
        def dec_or_state(s, ss):
            dst = lbuf.at[0, chunk(i)]
            rcopy(dst, dst, ss.at[s, i], rsem.at[s, i], sib).wait_send()

        @pl.when(is_even)
        def _():
            dec_or_state(L1, ssem)

        @pl.when(jnp.logical_or(z4 == 1, z4 == 2))
        def _():
            dec_or_state(L2, ssem)

        @pl.when((z == 3) | (z == 4) | (z == 0) | (z == 7))
        def _():
            dec_or_state(L3, ssem)

        @pl.when(z == 3)
        def _():
            dec_or_state(L3, ssem2)

        @pl.when(jnp.logical_and(x < NX - 1, (z != 3) & (z != 4)))
        def _():
            dec_or_state(TT, ssem)

        @pl.when(jnp.logical_and(x < NX - 1, z == 7))
        def _():
            dec_or_state(TT, ssem2)

        @pl.when(jnp.logical_not(x_odd))
        def _():
            dec_or_state(X4, ssem)

        @pl.when(x <= 1)
        def _():
            dec_or_state(X5, ssem)

        @pl.when(x == 1)
        def _():
            dec_or_state(X5, ssem2)

        def sib_done(s):
            dst = lbuf.at[0, chunk(i)]
            rcopy(dst, dst, sib_s.at[s, i], sib_r.at[s, i], sib).wait_send()

        @pl.when(jnp.logical_not(is_even))
        def _():
            sib_done(L1)

        @pl.when(z4 >= 2)
        def _():
            sib_done(L2)

        @pl.when(z >= 4)
        def _():
            sib_done(L3)

        @pl.when(x_odd)
        def _():
            sib_done(X4)

        @pl.when(x >= 2)
        def _():
            sib_done(X5)

        return 0

    lax.fori_loop(0, NC, drain, 0)

    def ddone(s, ss):
        dcopy(dec.at[0], 0, s, sib, ss).wait_send()

    @pl.when(is_even)
    def _():
        ddone(L1, ssem)

    @pl.when(jnp.logical_or(z4 == 1, z4 == 2))
    def _():
        ddone(L2, ssem)

    @pl.when((z == 3) | (z == 4) | (z == 0) | (z == 7))
    def _():
        ddone(L3, ssem)

    @pl.when(z == 3)
    def _():
        ddone(L3, ssem2)

    @pl.when(jnp.logical_and(x < NX - 1, (z != 3) & (z != 4)))
    def _():
        ddone(TT, ssem)

    @pl.when(jnp.logical_and(x < NX - 1, z == 7))
    def _():
        ddone(TT, ssem2)

    @pl.when(jnp.logical_not(x_odd))
    def _():
        ddone(X4, ssem)


def per_device(
    mixed_input,
    conv_weight,
    conv_bias,
    gate_input,
    log_decay,
    level_weights,
    skip_gain,
    norm_gain,
    seg_lengths,
):
    vmem = pl.BlockSpec(memory_space=pltpu.VMEM)
    smem = pl.BlockSpec(memory_space=pltpu.SMEM)
    dma = pltpu.SemaphoreType.DMA
    return pl.pallas_call(
        kernel,
        out_shape=jax.ShapeDtypeStruct((TOK, WIDTH), BF16),
        in_specs=[vmem] * 7 + [smem] * 2,
        out_specs=vmem,
        scratch_shapes=[
            pltpu.VMEM((HALO, CH), BF16),
            pltpu.VMEM((TOK + 8, BR), F32),
            pltpu.VMEM((WIDTH, TOK), BF16),
            pltpu.VMEM((TOK, STATE), BF16),
            pltpu.VMEM((TOK, STATE), BF16),
            pltpu.VMEM((WIDTH, STATE), F32),
            pltpu.VMEM((WIDTH, STATE), F32),
            pltpu.VMEM((HALF, STATE), F32),
            pltpu.VMEM((4, NC, XR, STATE), jnp.int16),
            pltpu.VMEM((5, 2 * NC, XR, STATE), jnp.int16),
            pltpu.VMEM((NC, XR, STATE), jnp.int16),
            pltpu.VMEM((5, HEADS, 128), F32),
            pltpu.VMEM((3, HEADS, 128), F32),
            pltpu.VMEM((2, HEADS, 128), F32),
            pltpu.VMEM((6, HEADS, 128), F32),
            pltpu.VMEM((HEADS, TOK), F32),
            pltpu.VMEM((TOK, 128), F32),
            pltpu.VMEM((HEADS, TOK), F32),
            pltpu.VMEM((HEADS, TOK), F32),
            pltpu.VMEM((TOK, TOK), F32),
            pltpu.VMEM((128, 128), jnp.int32),
            pltpu.VMEM((WIDTH, TOK), F32),
            pltpu.VMEM((WIDTH, TOK), F32),
            dma,
            dma,
            dma,
            dma,
            dma((NB,)),
            dma((NB,)),
            dma((6, NC + 1)),
            dma((6, NC + 1)),
            dma((6, NC + 1)),
            dma((6, NC)),
            dma((6, NC)),
        ],
        compiler_params=pltpu.CompilerParams(
            collective_id=0, has_side_effects=True, vmem_limit_bytes=60 * 1024 * 1024
        ),
        name="layer",
    )(
        mixed_input,
        gate_input,
        log_decay,
        level_weights,
        conv_weight,
        conv_bias.reshape(1, CH),
        norm_gain.reshape(1, WIDTH),
        skip_gain,
        seg_lengths,
    )


def solution(mesh):
    in_specs = (
        P(("batch", "group"), None),
        P(),
        P(),
        P(("batch", "group"), None),
        P(None, ("batch", "group")),
        P(None, None, ("batch", "group")),
        P(),
        P(),
        P("batch"),
    )
    out_specs = P(("batch", "group"), None)
    return jax.shard_map(
        per_device, mesh=mesh, in_specs=in_specs, out_specs=out_specs, check_vma=False
    )
```

time: 284 us -> 92 us (0.32)
  the two profiles are of different devices: /device:TPU:16 before, /device:TPU:151 now
where the time goes in v1:
time: 92 us; the launch traced here: 91.8 us
  Pallas kernels  84.3 us (92%)
  local copies, waits for them, and re-layouts  7.44 us (8%)
    pallas_call x1, Pallas kernels, per_device(): pl.pallas_call(kernel, out_shape=jax.ShapeDtypeStruct((TOK, WIDTH), BF16)...  84.3 us
    unnamed x2, local copies, waits for them, and re-layouts  4.82 us

profile of v1, /device:TPU:151, one launch (start us, length us, event | category | flops | bytes accessed | tf_op | source)
XLA Modules:
  0.0 91.8 jit_solution(7355259686469472612)
XLA Ops:
  0.0 1.3 %reshape.7.ng = f32[1,2560]{1,0:T(1,128)} reshape(f32[2560]{0:T(1024)} %param.16) | data formatting | bytes 20480 | tf_op jit(solution)/shard_map/reshape | solution.py:840
  1.3 1.3 %reshape.6.cb = f32[1,2816]{1,0:T(1,128)} reshape(f32[2816]{0:T(1024)} %param.11) | data formatting | bytes 22528 | tf_op jit(solution)/shard_map/reshape | solution.py:839
  2.6 2.4 %copy.10.lam = f32[40,20,256]{2,1,0:T(8,128)} copy(f32[40,20,256]{2,0,1:T(8,128)} %param.14) | data formatting | bytes 1638400 | tf_op args[5]
  5.0 84.3 %layer.1 = bf16[256,2560]{1,0:T(8,128)(2,1)} custom-call(bf16[256,2816]{1,0:T(8,128)(2,1)} %mixed.1, bf16[256,2560]{1,0:T(8,128)(2,1)} %gate.1, f32[40,256]{1,0:T(8,128)} %ld.1, f32[40,20,256]{2,1,0:T(8,128)} %copy.10.lam, f32[4,2816]{1,0:T(4,128)} %cw.1, f32[1,2816]{1,0:T(1,128)} %reshape.6.cb, f32[1,2560]{1,0:T(1,128)} %reshape.7.ng, f32[40]{0:T(128)} %skip.1, ...), custom_call_target="tpu_custom_call" | custom-call | tf_op jit(solution)/shard_map/layer/pallas_call | solution.py:788
  89.3 2.5 %copy.12 = bf16[256,2560]{1,0:T(8,128)(2,1)} copy(bf16[256,2560]{1,0:T(8,128)(2,1)} %layer.1) | data formatting | bytes 2621440

commit v2 on v1

v2 whole, which is shorter than its diff:
```python
import jax
import jax.numpy as jnp
from jax import lax
from jax.experimental import pallas as pl
from jax.experimental.pallas import tpu as pltpu
from jax.sharding import PartitionSpec as P

EPS = 1e-05
F32 = jnp.float32
BF16 = jnp.bfloat16
MESH = pl.DeviceIdType.MESH

TOK = 256
WIDTH = 2560
HEADS = 40
HD = 64
STATE = 128
CH = 2816
TAPS = 4
NX, NZ = 4, 8
HALF = WIDTH // 2
HALO = 16
PR = HALF // NZ
SG = 32
NSG = PR // SG
XP = PR + 16
PB = 2 * PR
NPB = WIDTH // PB
BR = 256
NB = WIDTH // BR
HPB = BR // HD
LOCAL_A = 8


def kernel(
    mixed_h,
    gate_h,
    ld,
    lam_h,
    cw,
    cb,
    ng,
    skip,
    segl,
    out,
    mixed,
    gate,
    lam,
    halo,
    pad,
    xst,
    keys,
    quer,
    ef,
    sibe,
    p1s,
    p1r,
    osnd,
    tr,
    lbuf,
    dtab,
    dline,
    theta,
    pbuf,
    cum,
    cumt,
    endw,
    entry,
    sct,
    lev,
    acc,
    gt,
    in_s,
    halo_s,
    halo_r,
    th_s,
    th_r,
    e_s,
    e_r,
    dz_s,
    dz_r,
    dx_s,
    dx_r,
    p1_s,
    p1_r,
    l_s,
    l_r,
    x_s,
    x_r,
    sib_s,
    sib_r,
):
    g = lax.axis_index("group")
    core = lax.rem(g, 2)
    z = lax.rem(g // 2, NZ)
    x = g // (2 * NZ)
    ngroups = 2 * NZ * NX

    def at(xx, zz, cc):
        return (xx * NZ + zz) * 2 + cc

    sib = at(x, z, 1 - core)
    gnext = lax.rem(g + 1, ngroups)
    gprev = lax.rem(g + ngroups - 1, ngroups)

    def zpeer(d):
        return lax.rem(z + d, NZ)

    def xpeer(d):
        return lax.rem(x + d, NX)

    barrier = pltpu.get_barrier_semaphore()

    def hello(peer):
        pl.semaphore_signal(barrier, inc=1, device_id={"group": peer}, device_id_type=MESH)

    for d in range(1, NZ):
        hello(at(x, zpeer(d), core))
    for d in range(1, NX):
        hello(at(xpeer(d), z, core))
    for peer in (sib, gnext, gprev):
        hello(peer)
    n_hello = NZ - 1 + NX - 1 + 3

    in_copies = [
        pltpu.make_async_copy(mixed_h, mixed, in_s.at[0]),
        pltpu.make_async_copy(lam_h, lam, in_s.at[1]),
        pltpu.make_async_copy(gate_h, gate, in_s.at[2]),
    ]
    for cp in in_copies:
        cp.start()

    def rcopy(src, dst, ss, rs, peer):
        return pltpu.make_async_remote_copy(
            src_ref=src,
            dst_ref=dst,
            send_sem=ss,
            recv_sem=rs,
            device_id={"group": peer},
            device_id_type=MESH,
        )

    first = g * TOK
    b1 = segl[0]
    b2 = segl[0] + segl[1]

    def seg_of(pos):
        s = (pos >= b1).astype(jnp.int32) + (pos >= b2).astype(jnp.int32)
        return jnp.where(pos >= 0, s, -1)

    lane_pos = first + lax.broadcasted_iota(jnp.int32, (8, TOK), 1)[0:1]
    seg_row = seg_of(lane_pos)
    last_row = seg_of(jnp.full((1, TOK), first + TOK - 1, jnp.int32))
    prev_row = seg_of(jnp.full((1, TOK), first - 1, jnp.int32))

    c = ld[...]
    lane = lax.broadcasted_iota(jnp.int32, (HEADS, TOK), 1)
    step = 1
    while step < TOK:
        c = c + jnp.where(lane >= step, pltpu.roll(c, step, 1), 0.0)
        step *= 2
    cum[...] = c
    c_end = c[:, TOK - 1 : TOK]
    endw[...] = jnp.exp(c_end - c) * (seg_row == last_row).astype(F32)
    entry[...] = jnp.exp(c) * (seg_row == prev_row).astype(F32)
    theta[0] = jnp.broadcast_to(jnp.exp(c_end), (HEADS, 128)) * (last_row == prev_row).astype(F32)[
        :, 0:128
    ]
    cpad = jnp.concatenate([c, jnp.zeros((128 - HEADS, TOK), F32)], axis=0)
    cumt[...] = jnp.concatenate([cpad[:, 0:128].T, cpad[:, 128:256].T], axis=0)

    si = lax.broadcasted_iota(jnp.int32, (128, 128), 0)
    ti = lax.broadcasted_iota(jnp.int32, (128, 128), 1)
    diff = si ^ ti
    lv = jnp.zeros((128, 128), jnp.int32)
    for b in range(7):
        lv = lv + (diff >= 2**b).astype(jnp.int32)
    lev[...] = lv

    in_copies[0].wait()
    pl.semaphore_wait(barrier, n_hello)

    halo_copy = rcopy(mixed.at[pl.ds(TOK - HALO, HALO)], halo, halo_s, halo_r, gnext)
    halo_copy.start()
    th_copy = rcopy(theta.at[0], theta.at[1], th_s, th_r, sib)
    th_copy.start()

    col_pos = first + lax.broadcasted_iota(jnp.int32, (TOK, 256), 0)
    seg_col = seg_of(col_pos)
    same = [None] + [seg_of(col_pos - t) == seg_col for t in range(1, TAPS)]

    def conv(cols):
        cur = mixed[:, cols].astype(F32)
        pad[8 : 8 + TOK, :] = cur
        pad[0:8, :] = halo[HALO - 8 : HALO, cols].astype(F32)
        total = cb[cols].reshape(1, BR) + cw[0:1, cols] * cur
        for t in range(1, TAPS):
            piece = pad[8 - t : 8 - t + TOK, :]
            total = total + cw[t : t + 1, cols] * jnp.where(same[t], piece, 0.0)
        return total * (1.0 / (1.0 + jnp.exp(-total)))

    halo_copy.wait_recv()
    kq = conv(pl.ds(WIDTH, 2 * STATE))
    keys[...] = kq[:, 0:STATE].astype(BF16)
    quer[...] = kq[:, STATE : 2 * STATE].astype(BF16)

    th_copy.wait_recv()
    dtab[z] = theta[0] * theta[1]

    def dz_copy(to, frm):
        return rcopy(dtab.at[frm], dtab.at[frm], dz_s.at[to], dz_r.at[frm], at(x, to, core))

    def dx_copy(to, frm):
        return rcopy(dline.at[frm], dline.at[frm], dx_s.at[to], dx_r.at[frm], at(to, z, core))

    def over_z(f):
        def go(d, _):
            f(zpeer(d))
            return 0

        lax.fori_loop(1, NZ, go, 0)

    def over_x(f):
        def go(d, _):
            f(xpeer(d))
            return 0

        lax.fori_loop(1, NX, go, 0)

    over_z(lambda o: dz_copy(o, z).start())

    def e_copy(i):
        rows = pl.ds(pl.multiple_of(i * BR, BR), BR)
        return rcopy(ef.at[rows], sibe.at[rows], e_s.at[i], e_r.at[i], sib)

    def conv_step(n, _):
        i = lax.rem(n + (1 - core) * (NB // 2), NB)
        base = pl.multiple_of(i * BR, BR)
        act = conv(pl.ds(base, BR)).T.astype(BF16)
        xst[pl.ds(base, BR), :] = act
        parts = []
        for j in range(HPB):
            w = endw[pl.ds(i * HPB + j, 1), :]
            parts.append((act[j * HD : (j + 1) * HD].astype(F32) * w).astype(BF16))
        e = jnp.dot(jnp.concatenate(parts, axis=0), keys[...], preferred_element_type=F32)
        ef[pl.ds(base, BR), :] = e
        e_copy(i).start()
        return 0

    lax.fori_loop(0, NB, conv_step, 0)

    xrow = lax.broadcasted_iota(jnp.int32, (16, 128), 0) // 3

    def encode(blocks):
        q = []
        ex = jnp.zeros((16, 128), F32)
        for k in range(NSG):
            top = jnp.max(jnp.abs(blocks[k]), axis=0, keepdims=True)
            e = jnp.ceil(jnp.log2(jnp.maximum(top, 1e-30))) - 14.0
            q.append(jnp.floor(blocks[k] * (1.0 / jnp.exp2(e)) + 0.5))
            ex = jnp.where(xrow == k, e, ex)
        return jnp.concatenate(q + [ex], axis=0).astype(jnp.int32).astype(jnp.int16)

    def decode(ref):
        ex = jnp.exp2(ref[PR:XP, :].astype(jnp.int32).astype(F32))
        return [
            ref[k * SG : (k + 1) * SG, :].astype(jnp.int32).astype(F32) * ex[3 * k : 3 * k + 1]
            for k in range(NSG)
        ]

    def head_of(o, k):
        return core * (HEADS // 2) + (o * NSG + k) // 2

    def p1_copy(to, frm):
        return rcopy(p1s.at[to], p1r.at[frm], p1_s.at[to], p1_r.at[frm], at(x, to, core))

    def wait_e(n, _):
        e_copy(core * (NB // 2) + n).wait_recv()
        return 0

    lax.fori_loop(0, NB // 2, wait_e, 0)

    def chip_step(n, _):
        o = lax.rem(z + NZ // 2 + n, NZ)
        blocks = []
        for k in range(NSG):
            rows = pl.ds(pl.multiple_of(core * HALF + o * PR + k * SG, SG), SG)
            own, other = ef[rows, :], sibe[rows, :]
            h = pl.ds(head_of(o, k), 1)
            low = jnp.where(core == 0, own, other)
            high = jnp.where(core == 0, other, own)
            d = jnp.where(core == 0, theta[1, h, :], theta[0, h, :])
            blocks.append(low * d + high)
        p1s[o] = encode(blocks)

        @pl.when(o != z)
        def _():
            p1_copy(o, z).start()

        @pl.when(o == z)
        def _():
            p1r[o] = p1s[o]

        return 0

    lax.fori_loop(0, NZ, chip_step, 0)

    over_z(lambda o: dz_copy(o, o).wait_recv())
    pair = [dtab[2 * j] * dtab[2 * j + 1] for j in range(NZ // 2)]
    quad = [pair[0] * pair[1], pair[2] * pair[3]]
    dline[x] = quad[0] * quad[1]
    over_x(lambda o: dx_copy(o, x).start())
    one = jnp.ones((HEADS, 128), F32)
    pbuf[1] = jnp.where(core == 1, theta[1], one)
    below = jnp.where(lax.rem(z, 2) == 1, dtab[jnp.maximum(z - 1, 0)], one)
    pbuf[2] = pbuf[1] * below
    pbuf[3] = pbuf[2] * jnp.where(
        lax.rem(z // 2, 2) == 1, jnp.where(z >= 4, pair[2], pair[0]), one
    )
    pbuf[4] = pbuf[3] * jnp.where(z >= 4, quad[0], one)

    s_t = lax.dot_general(
        keys[...], quer[...], (((1,), (1,)), ((), ())), preferred_element_type=F32
    )
    rowi = lax.broadcasted_iota(jnp.int32, (TOK, TOK), 0)
    coli = lax.broadcasted_iota(jnp.int32, (TOK, TOK), 1)
    ok = (rowi <= coli) & (seg_col == seg_row)
    sct[...] = jnp.where(ok, s_t, 0.0)

    def local_heads(i, _):
        rolled = pltpu.roll(cumt[...], lax.rem(128 - i * HPB, 128), 1)
        for j in range(HPB):
            h = i * HPB + j
            rows = pl.ds(pl.multiple_of(h * HD, HD), HD)
            ccol = rolled[:, j : j + 1]
            crow = cum[pl.ds(h, 1), :]

            def lam_row(l, lo):
                return lam[l, pl.ds(h, 1), :][:, lo : lo + 128]

            def picked(lo):
                p = jnp.broadcast_to(lam_row(7, lo), (128, 128))
                for l in range(7):
                    p = jnp.where(lev[...] == l, lam_row(l, lo), p)
                return p

            def mix(slo, tlo, pick):
                gap = crow[:, tlo : tlo + 128] - ccol[slo : slo + 128]
                decay = jnp.exp(jnp.minimum(gap, 0.0))
                return (sct[slo : slo + 128, tlo : tlo + 128] * pick * decay).astype(BF16)

            m00 = mix(0, 0, picked(0))
            m01 = mix(0, 128, lam_row(8, 128))
            m11 = mix(128, 128, picked(128))
            xs = xst[rows, :]
            left = jnp.dot(xs[:, 0:128], m00, preferred_element_type=F32)
            right = jnp.dot(xs, jnp.concatenate([m01, m11], axis=0), preferred_element_type=F32)
            acc[rows, :] = jnp.concatenate([left, right], axis=1) + skip[h] * xs.astype(F32)
        return 0

    in_copies[1].wait()
    lax.fori_loop(0, LOCAL_A, local_heads, 0)

    over_z(lambda o: p1_copy(o, o).wait_recv())
    cs = [decode(p1r.at[j]) for j in range(NZ)]
    b01, b45, b03, b07 = [], [], [], []
    for k in range(NSG):
        h = pl.ds(head_of(z, k), 1)
        d = [dtab[j, h, :] for j in range(NZ)]
        pr = [cs[2 * j][k] * d[2 * j + 1] + cs[2 * j + 1][k] for j in range(NZ // 2)]
        lo = pr[0] * (d[2] * d[3]) + pr[1]
        hi = pr[2] * (d[6] * d[7]) + pr[3]
        b01.append(pr[0])
        b45.append(pr[2])
        b03.append(lo)
        b07.append(lo * (d[4] * d[5] * d[6] * d[7]) + hi)
    osnd[3] = encode(b07)

    def x_copy(to, frm):
        return rcopy(osnd.at[3], tr.at[frm], x_s.at[to], x_r.at[frm], at(to, z, core))

    def send_x(o):
        @pl.when(o > x)
        def _():
            x_copy(o, x).start()

    over_x(send_x)
    osnd[2] = encode(b03)
    osnd[0] = encode(b01)
    osnd[1] = encode(b45)

    me = core * NZ + z

    def l_copy(lvl, src, o, frm):
        return rcopy(
            src, lbuf.at[lvl, core * NZ + frm], l_s.at[lvl, o], l_r.at[lvl, frm], at(x, o, core)
        )

    def sib_copy(lvl, o):
        dst = lbuf.at[lvl, core * NZ + o]
        return rcopy(dst, dst, sib_s.at[lvl, o], sib_r.at[lvl, o], sib)

    def sib_wait(lvl, o):
        dst = lbuf.at[lvl, (1 - core) * NZ + o]
        rcopy(dst, dst, sib_s.at[lvl, o], sib_r.at[lvl, o], sib).wait_recv()

    def bit(v, b):
        return lax.rem(v // 2**b, 2) == 1

    def keep(lvl, src):
        lbuf[lvl, me] = src
        sib_copy(lvl, z).start()

    def send_l3(o):
        @pl.when(o >= 4)
        def _():
            l_copy(2, osnd.at[2], o, z).start()

    def send_l2(o):
        @pl.when(bit(o, 1))
        def _():
            l_copy(1, osnd.at[o // 4], o, z).start()

    over_z(send_l3)
    over_z(send_l2)

    def l1_copy(o):
        return rcopy(
            p1s.at[o],
            lbuf.at[0, core * NZ + o],
            l_s.at[0, o],
            l_r.at[0, o],
            at(x, zpeer(1), core),
        )

    def send_l1(o, _):
        l1_copy(o).start()
        return 0

    @pl.when(lax.rem(z, 2) == 0)
    def _():
        lax.fori_loop(0, NZ, send_l1, 0)

    @pl.when(z >= 4)
    def _():
        keep(2, osnd[2])

    @pl.when(bit(z, 1))
    def _():
        keep(1, osnd[z // 4])

    lax.fori_loop(LOCAL_A, NB, local_heads, 0)

    over_x(lambda o: dx_copy(o, o).wait_recv())
    pbuf[5] = pbuf[4] * jnp.where(lax.rem(x, 2) == 1, dline[jnp.maximum(x - 1, 0)], one)

    def x_in(frm):
        x_copy(frm, frm).wait_recv()

    def send_l4(frm):
        over_z(lambda o: l_copy(3, tr.at[frm], o, z).start())
        keep(3, tr[frm])

    def send_l5():
        t0, t1 = decode(tr.at[0]), decode(tr.at[1])
        osnd[4] = encode(
            [t0[k] * dline[1, pl.ds(head_of(z, k), 1), :] + t1[k] for k in range(NSG)]
        )
        over_z(lambda o: l_copy(4, osnd.at[4], o, z).start())
        keep(4, osnd[4])

    @pl.when(x == 1)
    def _():
        x_in(0)
        send_l4(0)

    @pl.when(x == 3)
    def _():
        x_in(2)
        send_l4(2)

    @pl.when(x >= 2)
    def _():
        x_in(1)
        x_in(0)
        send_l5()

    def pass_on(lvl):
        def one_piece(o):
            l_copy(lvl, lbuf.at[lvl, me], o, o).wait_recv()
            sib_copy(lvl, o).start()

        over_z(one_piece)

    def sib_all(lvl):
        def go(o, _):
            sib_wait(lvl, o)
            return 0

        lax.fori_loop(0, NZ, go, 0)

    def far(level):
        def body(i, _):
            base = pl.multiple_of(i * PB, PB)
            if level == 0:
                state = sibe[pl.ds(base, PB), :].astype(BF16)
            else:
                parts = []
                for m in range(2):
                    v = decode(lbuf.at[level - 1, 2 * i + m])
                    for k in range(NSG):
                        p = pbuf[level, pl.ds(i * NSG + (m * NSG + k) // 2, 1), :]
                        parts.append((v[k] * p).astype(BF16))
                state = jnp.concatenate(parts, axis=0)
            read = lax.dot_general(
                state, quer[...], (((1,), (1,)), ((), ())), preferred_element_type=F32
            )
            for j in range(NSG):
                h = pl.ds(i * NSG + j, 1)
                coef = lam[9 + level, h, :] * entry[h, :]
                rows = pl.ds(pl.multiple_of(base + j * HD, HD), HD)
                acc[rows, :] = acc[rows, :] + read[j * HD : (j + 1) * HD] * coef
            return 0

        lax.fori_loop(0, NPB, body, 0)

    def gate_block(i, _):
        cols = pl.ds(pl.multiple_of(i * BR, BR), BR)
        v = gate[:, cols].astype(F32)
        gt[cols, :] = (v * (1.0 / (1.0 + jnp.exp(-v)))).T
        return 0

    in_copies[2].wait()
    lax.fori_loop(0, NB, gate_block, 0)

    def wait_e2(n, _):
        e_copy((1 - core) * (NB // 2) + n).wait_recv()
        return 0

    lax.fori_loop(0, NB // 2, wait_e2, 0)

    @pl.when(core == 1)
    def _():
        far(0)

    @pl.when(z >= 4)
    def _():
        pass_on(2)

    @pl.when(bit(z, 1))
    def _():
        pass_on(1)

    @pl.when(lax.rem(z, 2) == 1)
    def _():
        def go(o, _):
            l1_copy(o).wait_recv()
            sib_copy(0, o).start()
            return 0

        lax.fori_loop(0, NZ, go, 0)

    @pl.when(z >= 4)
    def _():
        sib_all(2)
        far(3)

    @pl.when(bit(z, 1))
    def _():
        sib_all(1)
        far(2)

    @pl.when(lax.rem(z, 2) == 1)
    def _():
        sib_all(0)
        far(1)

    @pl.when(lax.rem(x, 2) == 1)
    def _():
        pass_on(3)

    @pl.when(x >= 2)
    def _():
        pass_on(4)

    @pl.when(lax.rem(x, 2) == 1)
    def _():
        sib_all(3)
        far(4)

    @pl.when(x >= 2)
    def _():
        sib_all(4)
        far(5)

    def gate_step(i, ssq):
        rows = pl.ds(pl.multiple_of(i * BR, BR), BR)
        v = acc[rows, :] * gt[rows, :]
        acc[rows, :] = v
        return ssq + jnp.sum((v * v).reshape(BR // 8, 8, TOK), axis=0)

    ssq = lax.fori_loop(0, NB, gate_step, jnp.zeros((8, TOK), F32))
    scale = lax.rsqrt(jnp.sum(ssq, axis=0, keepdims=True) * (1.0 / WIDTH) + EPS)

    def out_step(i, _):
        cols = pl.ds(pl.multiple_of(i * BR, BR), BR)
        v = (acc[cols, :] * scale).T
        out[:, cols] = (v * ng[cols].reshape(1, BR)).astype(BF16)
        return 0

    lax.fori_loop(0, NB, out_step, 0)

    halo_copy.wait_send()
    th_copy.wait_send()

    def e_done(i, _):
        e_copy(i).wait_send()
        return 0

    lax.fori_loop(0, NB, e_done, 0)
    over_z(lambda o: dz_copy(o, z).wait_send())
    over_z(lambda o: p1_copy(o, z).wait_send())
    over_x(lambda o: dx_copy(o, x).wait_send())

    def x_done(o):
        @pl.when(o > x)
        def _():
            x_copy(o, x).wait_send()

    over_x(x_done)

    def l_done(o):
        @pl.when(o >= 4)
        def _():
            l_copy(2, osnd.at[2], o, z).wait_send()

        @pl.when(bit(o, 1))
        def _():
            l_copy(1, osnd.at[0], o, z).wait_send()

        @pl.when(lax.rem(x, 2) == 1)
        def _():
            l_copy(3, tr.at[0], o, z).wait_send()

        @pl.when(x >= 2)
        def _():
            l_copy(4, osnd.at[4], o, z).wait_send()

    over_z(l_done)

    def sib_done(lvl):
        def go(o, _):
            sib_copy(lvl, o).wait_send()
            return 0

        lax.fori_loop(0, NZ, go, 0)

    @pl.when(lax.rem(z, 2) == 0)
    def _():
        def go(o, _):
            l1_copy(o).wait_send()
            return 0

        lax.fori_loop(0, NZ, go, 0)

    pl.when(lax.rem(z, 2) == 1)(lambda: sib_done(0))
    pl.when(bit(z, 1))(lambda: sib_done(1))
    pl.when(z >= 4)(lambda: sib_done(2))
    pl.when(lax.rem(x, 2) == 1)(lambda: sib_done(3))
    pl.when(x >= 2)(lambda: sib_done(4))


def per_device(
    mixed_input,
    conv_weight,
    conv_bias,
    gate_input,
    log_decay,
    level_weights,
    skip_gain,
    norm_gain,
    seg_lengths,
):
    vmem = pl.BlockSpec(memory_space=pltpu.VMEM)
    hbm = pl.BlockSpec(memory_space=pl.ANY)
    smem = pl.BlockSpec(memory_space=pltpu.SMEM)
    dma = pltpu.SemaphoreType.DMA
    return pl.pallas_call(
        kernel,
        out_shape=jax.ShapeDtypeStruct((TOK, WIDTH), BF16),
        in_specs=[hbm, hbm, vmem, hbm] + [vmem] * 3 + [smem] * 2,
        out_specs=vmem,
        scratch_shapes=[
            pltpu.VMEM((TOK, CH), BF16),
            pltpu.VMEM((TOK, WIDTH), BF16),
            pltpu.VMEM((20, HEADS, TOK), F32),
            pltpu.VMEM((HALO, CH), BF16),
            pltpu.VMEM((TOK + 8, BR), F32),
            pltpu.VMEM((WIDTH, TOK), BF16),
            pltpu.VMEM((TOK, STATE), BF16),
            pltpu.VMEM((TOK, STATE), BF16),
            pltpu.VMEM((WIDTH, STATE), F32),
            pltpu.VMEM((WIDTH, STATE), F32),
            pltpu.VMEM((NZ, XP, STATE), jnp.int16),
            pltpu.VMEM((NZ, XP, STATE), jnp.int16),
            pltpu.VMEM((5, XP, STATE), jnp.int16),
            pltpu.VMEM((NX, XP, STATE), jnp.int16),
            pltpu.VMEM((5, 2 * NZ, XP, STATE), jnp.int16),
            pltpu.VMEM((NZ, HEADS, 128), F32),
            pltpu.VMEM((NX, HEADS, 128), F32),
            pltpu.VMEM((2, HEADS, 128), F32),
            pltpu.VMEM((6, HEADS, 128), F32),
            pltpu.VMEM((HEADS, TOK), F32),
            pltpu.VMEM((TOK, 128), F32),
            pltpu.VMEM((HEADS, TOK), F32),
            pltpu.VMEM((HEADS, TOK), F32),
            pltpu.VMEM((TOK, TOK), F32),
            pltpu.VMEM((128, 128), jnp.int32),
            pltpu.VMEM((WIDTH, TOK), F32),
            pltpu.VMEM((WIDTH, TOK), F32),
            dma((3,)),
            dma,
            dma,
            dma,
            dma,
            dma((NB,)),
            dma((NB,)),
            dma((NZ,)),
            dma((NZ,)),
            dma((NX,)),
            dma((NX,)),
            dma((NZ,)),
            dma((NZ,)),
            dma((5, NZ)),
            dma((5, NZ)),
            dma((NX,)),
            dma((NX,)),
            dma((5, NZ)),
            dma((5, NZ)),
        ],
        compiler_params=pltpu.CompilerParams(
            collective_id=0, has_side_effects=True, vmem_limit_bytes=60 * 1024 * 1024
        ),
        name="layer",
    )(
        mixed_input,
        gate_input,
        log_decay,
        jnp.transpose(level_weights, (1, 0, 2)),
        conv_weight,
        conv_bias,
        norm_gain,
        skip_gain,
        seg_lengths,
    )


def solution(mesh):
    in_specs = (
        P(("batch", "group"), None),
        P(),
        P(),
        P(("batch", "group"), None),
        P(None, ("batch", "group")),
        P(None, None, ("batch", "group")),
        P(),
        P(),
        P("batch"),
    )
    out_specs = P(("batch", "group"), None)
    return jax.shard_map(
        per_device, mesh=mesh, in_specs=in_specs, out_specs=out_specs, check_vma=False
    )
```

time: 92 us -> 74.3 us (0.81)
  the two profiles are of different devices: /device:TPU:151 before, /device:TPU:22 now
where the time goes in v2:
time: 74.3 us; the launch traced here: 74.1 us
  Pallas kernels  71.6 us (96%)
  local copies, waits for them, and re-layouts  2.46 us (3%)
    pallas_call x1, Pallas kernels, per_device(): pl.pallas_call(kernel, out_shape=jax.ShapeDtypeStruct((TOK, WIDTH), BF16)...  71.6 us
    unnamed x1, local copies, waits for them, and re-layouts  2.46 us

profile of v2, /device:TPU:22, one launch (start us, length us, event | category | flops | bytes accessed | tf_op | source)
XLA Modules:
  0.0 74.1 jit_solution(16027881184805652321)
XLA Ops:
  0.0 71.6 %layer.1 = bf16[256,2560]{1,0:T(8,128)(2,1)} custom-call(bf16[256,2816]{1,0:T(8,128)(2,1)} %mixed_h.1, bf16[256,2560]{1,0:T(8,128)(2,1)} %gate_h.1, f32[40,256]{1,0:T(8,128)} %ld.1, f32[20,40,256]{2,1,0:T(8,128)} %bitcast.1, f32[4,2816]{1,0:T(4,128)} %cw.1, f32[2816]{0:T(1024)} %cb.1, f32[2560]{0:T(1024)} %ng.1, f32[40]{0:T(128)} %skip.1, s32[3]{0:T(128)} %segl.1), custom_call_target="tpu_custom_call" | custom-call | tf_op jit(solution)/shard_map/layer/pallas_call | solution.py:688
  71.6 2.5 %copy.11 = bf16[256,2560]{1,0:T(8,128)(2,1)} copy(bf16[256,2560]{1,0:T(8,128)(2,1)} %layer.1) | data formatting | bytes 2621440

commit v3 on v2

--- a/solution.py
+++ b/solution.py
@@ -30,6 +30,7 @@
 NB = WIDTH // BR
 HPB = BR // HD
 LOCAL_A = 8
+CONV_A = 4
 
 
 def kernel(
@@ -48,6 +49,7 @@
     lam,
     halo,
     pad,
+    act,
     xst,
     keys,
     quer,
@@ -85,6 +87,10 @@
     p1_r,
     l_s,
     l_r,
+    r2_s,
+    r3_s,
+    r_s,
+    up_s,
     x_s,
     x_r,
     sib_s,
@@ -177,32 +183,43 @@
         lv = lv + (diff >= 2**b).astype(jnp.int32)
     lev[...] = lv
 
+    col_pos = first + lax.broadcasted_iota(jnp.int32, (TOK, 256), 0)
+    seg_col = seg_of(col_pos)
+    same = [None] + [seg_of(col_pos - t) == seg_col for t in range(1, TAPS)]
+
+    def taps(cols, rows, cur):
+        total = cb[cols].reshape(1, BR) + cw[0:1, cols] * cur
+        for t in range(1, TAPS):
+            piece = pad[8 - t : 8 - t + rows, :]
+            total = total + cw[t : t + 1, cols] * jnp.where(same[t][0:rows], piece, 0.0)
+        return total * (1.0 / (1.0 + jnp.exp(-total)))
+
+    pad[0:8, :] = jnp.zeros((8, BR), F32)
+
+    def conv_rows(i, _):
+        cols = pl.ds(pl.multiple_of(i * BR, BR), BR)
+        cur = mixed[:, cols].astype(F32)
+        pad[8 : 8 + TOK, :] = cur
+        act[:, cols] = taps(cols, TOK, cur)
+        return 0
+
+    def conv_first(i, _):
+        cols = pl.ds(pl.multiple_of(i * BR, BR), BR)
+        cur = mixed[0:16, cols].astype(F32)[0:8]
+        pad[8:16, :] = cur
+        pad[0:8, :] = halo[:, cols].astype(F32)[8:16]
+        act[0:8, cols] = taps(cols, 8, cur)
+        return 0
+
     in_copies[0].wait()
+    lax.fori_loop(0, CONV_A, conv_rows, 0)
     pl.semaphore_wait(barrier, n_hello)
 
     halo_copy = rcopy(mixed.at[pl.ds(TOK - HALO, HALO)], halo, halo_s, halo_r, gnext)
     halo_copy.start()
     th_copy = rcopy(theta.at[0], theta.at[1], th_s, th_r, sib)
     th_copy.start()
-
-    col_pos = first + lax.broadcasted_iota(jnp.int32, (TOK, 256), 0)
-    seg_col = seg_of(col_pos)
-    same = [None] + [seg_of(col_pos - t) == seg_col for t in range(1, TAPS)]
-
-    def conv(cols):
-        cur = mixed[:, cols].astype(F32)
-        pad[8 : 8 + TOK, :] = cur
-        pad[0:8, :] = halo[HALO - 8 : HALO, cols].astype(F32)
-        total = cb[cols].reshape(1, BR) + cw[0:1, cols] * cur
-        for t in range(1, TAPS):
-            piece = pad[8 - t : 8 - t + TOK, :]
-            total = total + cw[t : t + 1, cols] * jnp.where(same[t], piece, 0.0)
-        return total * (1.0 / (1.0 + jnp.exp(-total)))
-
-    halo_copy.wait_recv()
-    kq = conv(pl.ds(WIDTH, 2 * STATE))
-    keys[...] = kq[:, 0:STATE].astype(BF16)
-    quer[...] = kq[:, STATE : 2 * STATE].astype(BF16)
+    lax.fori_loop(CONV_A, CH // BR, conv_rows, 0)
 
     th_copy.wait_recv()
     dtab[z] = theta[0] * theta[1]
@@ -229,6 +246,11 @@
 
     over_z(lambda o: dz_copy(o, z).start())
 
+    halo_copy.wait_recv()
+    lax.fori_loop(0, CH // BR, conv_first, 0)
+    keys[...] = act[:, WIDTH : WIDTH + STATE].astype(BF16)
+    quer[...] = act[:, WIDTH + STATE : CH].astype(BF16)
+
     def e_copy(i):
         rows = pl.ds(pl.multiple_of(i * BR, BR), BR)
         return rcopy(ef.at[rows], sibe.at[rows], e_s.at[i], e_r.at[i], sib)
@@ -236,12 +258,12 @@
     def conv_step(n, _):
         i = lax.rem(n + (1 - core) * (NB // 2), NB)
         base = pl.multiple_of(i * BR, BR)
-        act = conv(pl.ds(base, BR)).T.astype(BF16)
-        xst[pl.ds(base, BR), :] = act
+        xt = act[:, pl.ds(base, BR)].T.astype(BF16)
+        xst[pl.ds(base, BR), :] = xt
         parts = []
         for j in range(HPB):
             w = endw[pl.ds(i * HPB + j, 1), :]
-            parts.append((act[j * HD : (j + 1) * HD].astype(F32) * w).astype(BF16))
+            parts.append((xt[j * HD : (j + 1) * HD].astype(F32) * w).astype(BF16))
         e = jnp.dot(jnp.concatenate(parts, axis=0), keys[...], preferred_element_type=F32)
         ef[pl.ds(base, BR), :] = e
         e_copy(i).start()
@@ -270,6 +292,12 @@
 
     def head_of(o, k):
         return core * (HEADS // 2) + (o * NSG + k) // 2
+
+    over_z(lambda o: dz_copy(o, o).wait_recv())
+    pair = [dtab[2 * j] * dtab[2 * j + 1] for j in range(NZ // 2)]
+    quad = [pair[0] * pair[1], pair[2] * pair[3]]
+    dline[x] = quad[0] * quad[1]
+    over_x(lambda o: dx_copy(o, x).start())
 
     def p1_copy(to, frm):
         return rcopy(p1s.at[to], p1r.at[frm], p1_s.at[to], p1_r.at[frm], at(x, to, core))
@@ -305,11 +333,47 @@
 
     lax.fori_loop(0, NZ, chip_step, 0)
 
-    over_z(lambda o: dz_copy(o, o).wait_recv())
+    s_t = lax.dot_general(
+        keys[...], quer[...], (((1,), (1,)), ((), ())), preferred_element_type=F32
+    )
+    rowi = lax.broadcasted_iota(jnp.int32, (TOK, TOK), 0)
+    coli = lax.broadcasted_iota(jnp.int32, (TOK, TOK), 1)
+    ok = (rowi <= coli) & (seg_col == seg_row)
+    sct[...] = jnp.where(ok, s_t, 0.0)
+
+    def local_heads(i, _):
+        rolled = pltpu.roll(cumt[...], lax.rem(128 - i * HPB, 128), 1)
+        for j in range(HPB):
+            h = i * HPB + j
+            rows = pl.ds(pl.multiple_of(h * HD, HD), HD)
+            ccol = rolled[:, j : j + 1]
+            crow = cum[pl.ds(h, 1), :]
+
+            def lam_row(l, lo):
+                return lam[l, pl.ds(h, 1), :][:, lo : lo + 128]
+
+            def picked(lo):
+                p = jnp.broadcast_to(lam_row(7, lo), (128, 128))
+                for l in range(7):
+                    p = jnp.where(lev[...] == l, lam_row(l, lo), p)
+                return p
+
+            def mix(slo, tlo, pick):
+                gap = crow[:, tlo : tlo + 128] - ccol[slo : slo + 128]
+                decay = jnp.exp(jnp.minimum(gap, 0.0))
+                return (sct[slo : slo + 128, tlo : tlo + 128] * pick * decay).astype(BF16)
+
+            m00 = mix(0, 0, picked(0))
+            m01 = mix(0, 128, lam_row(8, 128))
+            m11 = mix(128, 128, picked(128))
+            xs = xst[rows, :]
+            left = jnp.dot(xs[:, 0:128], m00, preferred_element_type=F32)
+            right = jnp.dot(xs, jnp.concatenate([m01, m11], axis=0), preferred_element_type=F32)
+            acc[rows, :] = jnp.concatenate([left, right], axis=1) + skip[h] * xs.astype(F32)
+        return 0
+
     pair = [dtab[2 * j] * dtab[2 * j + 1] for j in range(NZ // 2)]
     quad = [pair[0] * pair[1], pair[2] * pair[3]]
-    dline[x] = quad[0] * quad[1]
-    over_x(lambda o: dx_copy(o, x).start())
     one = jnp.ones((HEADS, 128), F32)
     pbuf[1] = jnp.where(core == 1, theta[1], one)
     below = jnp.where(lax.rem(z, 2) == 1, dtab[jnp.maximum(z - 1, 0)], one)
@@ -318,45 +382,6 @@
         lax.rem(z // 2, 2) == 1, jnp.where(z >= 4, pair[2], pair[0]), one
     )
     pbuf[4] = pbuf[3] * jnp.where(z >= 4, quad[0], one)
-
-    s_t = lax.dot_general(
-        keys[...], quer[...], (((1,), (1,)), ((), ())), preferred_element_type=F32
-    )
-    rowi = lax.broadcasted_iota(jnp.int32, (TOK, TOK), 0)
-    coli = lax.broadcasted_iota(jnp.int32, (TOK, TOK), 1)
-    ok = (rowi <= coli) & (seg_col == seg_row)
-    sct[...] = jnp.where(ok, s_t, 0.0)
-
-    def local_heads(i, _):
-        rolled = pltpu.roll(cumt[...], lax.rem(128 - i * HPB, 128), 1)
-        for j in range(HPB):
-            h = i * HPB + j
-            rows = pl.ds(pl.multiple_of(h * HD, HD), HD)
-            ccol = rolled[:, j : j + 1]
-            crow = cum[pl.ds(h, 1), :]
-
-            def lam_row(l, lo):
-                return lam[l, pl.ds(h, 1), :][:, lo : lo + 128]
-
-            def picked(lo):
-                p = jnp.broadcast_to(lam_row(7, lo), (128, 128))
-                for l in range(7):
-                    p = jnp.where(lev[...] == l, lam_row(l, lo), p)
-                return p
-
-            def mix(slo, tlo, pick):
-                gap = crow[:, tlo : tlo + 128] - ccol[slo : slo + 128]
-                decay = jnp.exp(jnp.minimum(gap, 0.0))
-                return (sct[slo : slo + 128, tlo : tlo + 128] * pick * decay).astype(BF16)
-
-            m00 = mix(0, 0, picked(0))
-            m01 = mix(0, 128, lam_row(8, 128))
-            m11 = mix(128, 128, picked(128))
-            xs = xst[rows, :]
-            left = jnp.dot(xs[:, 0:128], m00, preferred_element_type=F32)
-            right = jnp.dot(xs, jnp.concatenate([m01, m11], axis=0), preferred_element_type=F32)
-            acc[rows, :] = jnp.concatenate([left, right], axis=1) + skip[h] * xs.astype(F32)
-        return 0
 
     in_copies[1].wait()
     lax.fori_loop(0, LOCAL_A, local_heads, 0)
@@ -379,8 +404,11 @@
     def x_copy(to, frm):
         return rcopy(osnd.at[3], tr.at[frm], x_s.at[to], x_r.at[frm], at(to, z, core))
 
+    def x_to(o):
+        return (o > x) & ((o < 3) | (x == 2))
+
     def send_x(o):
-        @pl.when(o > x)
+        @pl.when(x_to(o))
         def _():
             x_copy(o, x).start()
 
@@ -411,18 +439,107 @@
         lbuf[lvl, me] = src
         sib_copy(lvl, z).start()
 
-    def send_l3(o):
-        @pl.when(o >= 4)
-        def _():
-            l_copy(2, osnd.at[2], o, z).start()
-
-    def send_l2(o):
-        @pl.when(bit(o, 1))
-        def _():
-            l_copy(1, osnd.at[o // 4], o, z).start()
-
-    over_z(send_l3)
-    over_z(send_l2)
+    def mir(o):
+        return jnp.where(z >= 6, lax.rem(11 - o, NZ), o)
+
+    l3_to = jnp.where(z >= 2, 4, 7)
+    l3_end = (z == 4) | (z == 7)
+    l3_mid = (z == 5) | (z == 6)
+
+    def l3_own(do):
+        @pl.when(z < 4)
+        def _():
+            do(lambda: l_copy(2, osnd.at[2], l3_to, z))
+
+        @pl.when(z >= 4)
+        def _():
+            do(lambda: l_copy(2, osnd.at[2], jnp.where(l3_end, mir(5), mir(4)), z))
+            do(lambda: l_copy(2, osnd.at[2], mir(6), z))
+
+    def l3_on(slot, o, to):
+        dst = lbuf.at[2, core * NZ + o]
+        return rcopy(dst, dst, r3_s.at[slot, o], l_r.at[2, o], at(x, to, core))
+
+    def l3_in(o):
+        l_copy(2, lbuf.at[2, me], o, o).wait_recv()
+
+    def l3_first():
+        @pl.when(l3_end)
+        def _():
+            for q in (3, 2):
+                o = mir(q)
+                l3_in(o)
+                l3_on(0, o, mir(5)).start()
+                l3_on(1, o, mir(6)).start()
+                sib_copy(2, o).start()
+
+    def l3_rest():
+        @pl.when(l3_mid)
+        def _():
+            for q in (6, 7, 0, 1):
+                o = mir(q)
+                l3_in(o)
+                l3_on(0, o, mir(4)).start()
+                sib_copy(2, o).start()
+            for q in (4, 3, 2):
+                o = mir(q)
+                l3_in(o)
+                sib_copy(2, o).start()
+
+        @pl.when(l3_end)
+        def _():
+            for q in (5, 6, 7, 0, 1):
+                o = mir(q)
+                l3_in(o)
+                sib_copy(2, o).start()
+
+    def l3_on_done():
+        @pl.when(l3_end)
+        def _():
+            for q in (3, 2):
+                l3_on(0, mir(q), mir(5)).wait_send()
+                l3_on(1, mir(q), mir(6)).wait_send()
+
+        @pl.when(l3_mid)
+        def _():
+            for q in (6, 7, 0, 1):
+                l3_on(0, mir(q), mir(4)).wait_send()
+
+    def l2_own(do):
+        for p in (2, 6):
+            r = lax.rem(z + NZ - p, NZ)
+            to = jnp.where((r == 1) | (r >= 5), p, p + 1)
+            do(lambda to=to, p=p: l_copy(1, osnd.at[p // 4], to, z))
+
+    l2_other = jnp.where(lax.rem(z, 2) == 0, z + 1, z - 1)
+
+    def l2_off(d):
+        return lax.rem(jnp.where(lax.rem(z, 2) == 0, z + NZ - d, z + d), NZ)
+
+    def l2_on(o):
+        dst = lbuf.at[1, core * NZ + o]
+        return rcopy(dst, dst, r2_s.at[o], l_r.at[1, o], at(x, l2_other, core))
+
+    def l2_in(o):
+        l_copy(1, lbuf.at[1, me], o, o).wait_recv()
+
+    def l2_first():
+        @pl.when(bit(z, 1))
+        def _():
+            for d in (1, 2, 3):
+                l2_in(l2_off(d))
+                l2_on(l2_off(d)).start()
+                sib_copy(1, l2_off(d)).start()
+
+    def l2_rest():
+        @pl.when(bit(z, 1))
+        def _():
+            for d in (7, 6, 5, 4):
+                l2_in(l2_off(d))
+                sib_copy(1, l2_off(d)).start()
+
+    l3_own(lambda c: c().start())
+    l2_own(lambda c: c().start())
 
     def l1_copy(o):
         return rcopy(
@@ -448,49 +565,6 @@
     @pl.when(bit(z, 1))
     def _():
         keep(1, osnd[z // 4])
-
-    lax.fori_loop(LOCAL_A, NB, local_heads, 0)
-
-    over_x(lambda o: dx_copy(o, o).wait_recv())
-    pbuf[5] = pbuf[4] * jnp.where(lax.rem(x, 2) == 1, dline[jnp.maximum(x - 1, 0)], one)
-
-    def x_in(frm):
-        x_copy(frm, frm).wait_recv()
-
-    def send_l4(frm):
-        over_z(lambda o: l_copy(3, tr.at[frm], o, z).start())
-        keep(3, tr[frm])
-
-    def send_l5():
-        t0, t1 = decode(tr.at[0]), decode(tr.at[1])
-        osnd[4] = encode(
-            [t0[k] * dline[1, pl.ds(head_of(z, k), 1), :] + t1[k] for k in range(NSG)]
-        )
-        over_z(lambda o: l_copy(4, osnd.at[4], o, z).start())
-        keep(4, osnd[4])
-
-    @pl.when(x == 1)
-    def _():
-        x_in(0)
-        send_l4(0)
-
-    @pl.when(x == 3)
-    def _():
-        x_in(2)
-        send_l4(2)
-
-    @pl.when(x >= 2)
-    def _():
-        x_in(1)
-        x_in(0)
-        send_l5()
-
-    def pass_on(lvl):
-        def one_piece(o):
-            l_copy(lvl, lbuf.at[lvl, me], o, o).wait_recv()
-            sib_copy(lvl, o).start()
-
-        over_z(one_piece)
 
     def sib_all(lvl):
         def go(o, _):
@@ -530,6 +604,7 @@
         gt[cols, :] = (v * (1.0 / (1.0 + jnp.exp(-v)))).T
         return 0
 
+    lax.fori_loop(LOCAL_A, NB, local_heads, 0)
     in_copies[2].wait()
     lax.fori_loop(0, NB, gate_block, 0)
 
@@ -543,13 +618,101 @@
     def _():
         far(0)
 
-    @pl.when(z >= 4)
-    def _():
-        pass_on(2)
-
-    @pl.when(bit(z, 1))
-    def _():
-        pass_on(1)
+    over_x(lambda o: dx_copy(o, o).wait_recv())
+    pbuf[5] = pbuf[4] * jnp.where(lax.rem(x, 2) == 1, dline[jnp.maximum(x - 1, 0)], one)
+
+    def x_in(frm):
+        x_copy(frm, frm).wait_recv()
+
+    NEAR = (2, 6, 1, 7)
+
+    def spread(lvl, src):
+        for d in NEAR:
+            l_copy(lvl, src, zpeer(d), z).start()
+
+    def r_copy(lvl, d, frm):
+        dst = lbuf.at[lvl, core * NZ + frm]
+        to = zpeer(d)
+        return rcopy(dst, dst, r_s.at[to], l_r.at[lvl, frm], at(x, to, core))
+
+    z_odd = lax.rem(z, 2) == 1
+
+    def up_copy(src, frm):
+        return rcopy(
+            src, lbuf.at[4, core * NZ + frm], up_s.at[frm], l_r.at[4, frm], at(xpeer(1), z, core)
+        )
+
+    def gather(lvl, up):
+        def arrived(frm):
+            l_copy(lvl, lbuf.at[lvl, me], frm, frm).wait_recv()
+
+        def hand_on(frm):
+            sib_copy(lvl, frm).start()
+            if up:
+                up_copy(lbuf.at[lvl, core * NZ + frm], frm).start()
+
+        def pull(d):
+            arrived(zpeer(d))
+            hand_on(zpeer(d))
+
+        arrived(zpeer(6))
+        r_copy(lvl, 1, zpeer(6)).start()
+
+        @pl.when(jnp.logical_not(z_odd))
+        def _():
+            r_copy(lvl, 2, zpeer(6)).start()
+
+        hand_on(zpeer(6))
+        arrived(zpeer(2))
+        r_copy(lvl, 7, zpeer(2)).start()
+
+        @pl.when(z_odd)
+        def _():
+            r_copy(lvl, 6, zpeer(2)).start()
+
+        hand_on(zpeer(2))
+        for d in (1, 7, 3, 5, 4):
+            pull(d)
+
+    def send_l4(frm):
+        spread(3, tr.at[frm])
+        keep(3, tr[frm])
+
+    def send_l5():
+        t0, t1 = decode(tr.at[0]), decode(tr.at[1])
+        osnd[4] = encode(
+            [t0[k] * dline[1, pl.ds(head_of(z, k), 1), :] + t1[k] for k in range(NSG)]
+        )
+        spread(4, osnd.at[4])
+        up_copy(osnd.at[4], z).start()
+        keep(4, osnd[4])
+
+    @pl.when(x == 1)
+    def _():
+        x_in(0)
+        send_l4(0)
+
+    @pl.when(x == 3)
+    def _():
+        x_in(2)
+        send_l4(2)
+
+    @pl.when(x == 2)
+    def _():
+        x_in(1)
+        x_in(0)
+        send_l5()
+
+    l3_first()
+    l2_first()
+
+    @pl.when(lax.rem(x, 2) == 1)
+    def _():
+        gather(3, False)
+
+    @pl.when(x == 2)
+    def _():
+        gather(4, True)
 
     @pl.when(lax.rem(z, 2) == 1)
     def _():
@@ -560,28 +723,32 @@
 
         lax.fori_loop(0, NZ, go, 0)
 
+    l3_rest()
+    l2_rest()
+
+    @pl.when(lax.rem(z, 2) == 1)
+    def _():
+        sib_all(0)
+        far(1)
+
+    @pl.when(bit(z, 1))
+    def _():
+        sib_all(1)
+        far(2)
+
     @pl.when(z >= 4)
     def _():
         sib_all(2)
         far(3)
 
-    @pl.when(bit(z, 1))
-    def _():
-        sib_all(1)
-        far(2)
-
-    @pl.when(lax.rem(z, 2) == 1)
-    def _():
-        sib_all(0)
-        far(1)
-
-    @pl.when(lax.rem(x, 2) == 1)
-    def _():
-        pass_on(3)
-
-    @pl.when(x >= 2)
-    def _():
-        pass_on(4)
+    @pl.when(x == 3)
+    def _():
+        def go(o, _):
+            up_copy(osnd.at[4], o).wait_recv()
+            sib_copy(4, o).start()
+            return 0
+
+        lax.fori_loop(0, NZ, go, 0)
 
     @pl.when(lax.rem(x, 2) == 1)
     def _():
@@ -623,30 +790,46 @@
     over_x(lambda o: dx_copy(o, x).wait_send())
 
     def x_done(o):
-        @pl.when(o > x)
+        @pl.when(x_to(o))
         def _():
             x_copy(o, x).wait_send()
 
     over_x(x_done)
 
-    def l_done(o):
-        @pl.when(o >= 4)
-        def _():
-            l_copy(2, osnd.at[2], o, z).wait_send()
-
-        @pl.when(bit(o, 1))
-        def _():
-            l_copy(1, osnd.at[0], o, z).wait_send()
-
-        @pl.when(lax.rem(x, 2) == 1)
-        def _():
-            l_copy(3, tr.at[0], o, z).wait_send()
-
-        @pl.when(x >= 2)
-        def _():
-            l_copy(4, osnd.at[4], o, z).wait_send()
-
-    over_z(l_done)
+    l3_own(lambda c: c().wait_send())
+    l3_on_done()
+    l2_own(lambda c: c().wait_send())
+
+    @pl.when(bit(z, 1))
+    def _():
+        for d in (1, 2, 3):
+            l2_on(l2_off(d)).wait_send()
+
+    def spread_done(lvl):
+        for d in NEAR:
+            l_copy(lvl, osnd.at[4], zpeer(d), z).wait_send()
+        for d in (1, 7):
+            r_copy(lvl, d, z).wait_send()
+
+        @pl.when(jnp.logical_not(z_odd))
+        def _():
+            r_copy(lvl, 2, z).wait_send()
+
+        @pl.when(z_odd)
+        def _():
+            r_copy(lvl, 6, z).wait_send()
+
+    pl.when(lax.rem(x, 2) == 1)(lambda: spread_done(3))
+
+    @pl.when(x == 2)
+    def _():
+        spread_done(4)
+
+        def go(o, _):
+            up_copy(osnd.at[4], o).wait_send()
+            return 0
+
+        lax.fori_loop(0, NZ, go, 0)
 
     def sib_done(lvl):
         def go(o, _):
@@ -696,6 +879,7 @@
             pltpu.VMEM((20, HEADS, TOK), F32),
             pltpu.VMEM((HALO, CH), BF16),
             pltpu.VMEM((TOK + 8, BR), F32),
+            pltpu.VMEM((TOK, CH), F32),
             pltpu.VMEM((WIDTH, TOK), BF16),
             pltpu.VMEM((TOK, STATE), BF16),
             pltpu.VMEM((TOK, STATE), BF16),
@@ -733,6 +917,10 @@
             dma((NZ,)),
             dma((5, NZ)),
             dma((5, NZ)),
+            dma((NZ,)),
+            dma((2, NZ)),
+            dma((NZ,)),
+            dma((NZ,)),
             dma((NX,)),
             dma((NX,)),
             dma((5, NZ)),

time: 74.3 us -> 64.5 us (0.87)
  the two profiles are of different devices: /device:TPU:22 before, /device:TPU:238 now
where the time goes in v3:
time: 64.5 us; the launch traced here: 64.3 us
  Pallas kernels  61.8 us (96%)
  local copies, waits for them, and re-layouts  2.46 us (4%)
    pallas_call x1, Pallas kernels, per_device(): pl.pallas_call(kernel, out_shape=jax.ShapeDtypeStruct((TOK, WIDTH), BF16)...  61.8 us
    unnamed x1, local copies, waits for them, and re-layouts  2.46 us

profile of v3, /device:TPU:238, one launch (start us, length us, event | category | flops | bytes accessed | tf_op | source)
XLA Modules:
  0.0 64.3 jit_solution(13839366470531218818)
XLA Ops:
  0.0 61.8 %layer.1 = bf16[256,2560]{1,0:T(8,128)(2,1)} custom-call(bf16[256,2816]{1,0:T(8,128)(2,1)} %mixed_h.1, bf16[256,2560]{1,0:T(8,128)(2,1)} %gate_h.1, f32[40,256]{1,0:T(8,128)} %ld.1, f32[20,40,256]{2,1,0:T(8,128)} %bitcast.1, f32[4,2816]{1,0:T(4,128)} %cw.1, f32[2816]{0:T(1024)} %cb.1, f32[2560]{0:T(1024)} %ng.1, f32[40]{0:T(128)} %skip.1, s32[3]{0:T(128)} %segl.1), custom_call_target="tpu_custom_call" | custom-call | tf_op jit(solution)/shard_map/layer/pallas_call | solution.py:871
  61.8 2.5 %copy.11 = bf16[256,2560]{1,0:T(8,128)(2,1)} copy(bf16[256,2560]{1,0:T(8,128)(2,1)} %layer.1) | data formatting | bytes 2621440

commit v4 on v3

--- a/solution.py
+++ b/solution.py
@@ -87,6 +87,7 @@
     p1_r,
     l_s,
     l_r,
+    l1_s,
     r2_s,
     r3_s,
     r_s,
@@ -251,25 +252,36 @@
     keys[...] = act[:, WIDTH : WIDTH + STATE].astype(BF16)
     quer[...] = act[:, WIDTH + STATE : CH].astype(BF16)
 
+    def turn(i, _):
+        base = pl.multiple_of(i * BR, BR)
+        xst[pl.ds(base, BR), :] = act[:, pl.ds(base, BR)].T.astype(BF16)
+        return 0
+
+    lax.fori_loop(0, NB, turn, 0)
+
     def e_copy(i):
-        rows = pl.ds(pl.multiple_of(i * BR, BR), BR)
+        rows = pl.ds(pl.multiple_of(i * PB, PB), PB)
         return rcopy(ef.at[rows], sibe.at[rows], e_s.at[i], e_r.at[i], sib)
 
-    def conv_step(n, _):
-        i = lax.rem(n + (1 - core) * (NB // 2), NB)
-        base = pl.multiple_of(i * BR, BR)
-        xt = act[:, pl.ds(base, BR)].T.astype(BF16)
-        xst[pl.ds(base, BR), :] = xt
+    def e_block(which, n):
+        return which * (NPB // 2) + lax.rem(n + z // 2 + 2, NPB // 2)
+
+    def e_step(i):
+        base = pl.multiple_of(i * PB, PB)
         parts = []
-        for j in range(HPB):
-            w = endw[pl.ds(i * HPB + j, 1), :]
-            parts.append((xt[j * HD : (j + 1) * HD].astype(F32) * w).astype(BF16))
+        for j in range(NSG):
+            w = endw[pl.ds(i * NSG + j, 1), :]
+            xt = xst[pl.ds(pl.multiple_of(base + j * HD, HD), HD), :]
+            parts.append((xt.astype(F32) * w).astype(BF16))
         e = jnp.dot(jnp.concatenate(parts, axis=0), keys[...], preferred_element_type=F32)
-        ef[pl.ds(base, BR), :] = e
+        ef[pl.ds(base, PB), :] = e
         e_copy(i).start()
+
+    def e_other(n, _):
+        e_step(e_block(1 - core, n))
         return 0
 
-    lax.fori_loop(0, NB, conv_step, 0)
+    lax.fori_loop(0, NPB // 2, e_other, 0)
 
     xrow = lax.broadcasted_iota(jnp.int32, (16, 128), 0) // 3
 
@@ -293,23 +305,10 @@
     def head_of(o, k):
         return core * (HEADS // 2) + (o * NSG + k) // 2
 
-    over_z(lambda o: dz_copy(o, o).wait_recv())
-    pair = [dtab[2 * j] * dtab[2 * j + 1] for j in range(NZ // 2)]
-    quad = [pair[0] * pair[1], pair[2] * pair[3]]
-    dline[x] = quad[0] * quad[1]
-    over_x(lambda o: dx_copy(o, x).start())
-
     def p1_copy(to, frm):
         return rcopy(p1s.at[to], p1r.at[frm], p1_s.at[to], p1_r.at[frm], at(x, to, core))
 
-    def wait_e(n, _):
-        e_copy(core * (NB // 2) + n).wait_recv()
-        return 0
-
-    lax.fori_loop(0, NB // 2, wait_e, 0)
-
-    def chip_step(n, _):
-        o = lax.rem(z + NZ // 2 + n, NZ)
+    def chip_step(o):
         blocks = []
         for k in range(NSG):
             rows = pl.ds(pl.multiple_of(core * HALF + o * PR + k * SG, SG), SG)
@@ -329,9 +328,43 @@
         def _():
             p1r[o] = p1s[o]
 
+    def e_mine(n, _):
+        i = e_block(core, n)
+        e_step(i)
+        e_copy(i).wait_recv()
+        for m in range(2):
+            chip_step(2 * lax.rem(n + z // 2 + 2, NPB // 2) + m)
         return 0
 
-    lax.fori_loop(0, NZ, chip_step, 0)
+    lax.fori_loop(0, NPB // 2, e_mine, 0)
+
+    over_z(lambda o: dz_copy(o, o).wait_recv())
+    pair = [dtab[2 * j] * dtab[2 * j + 1] for j in range(NZ // 2)]
+    quad = [pair[0] * pair[1], pair[2] * pair[3]]
+    dline[x] = quad[0] * quad[1]
+    over_x(lambda o: dx_copy(o, x).start())
+
+
+    me = core * NZ + z
+
+    def l_copy(lvl, src, o, frm):
+        return rcopy(
+            src, lbuf.at[lvl, core * NZ + frm], l_s.at[lvl, o], l_r.at[lvl, frm], at(x, o, core)
+        )
+
+    def l1_copy(o):
+        return rcopy(
+            p1s.at[o],
+            lbuf.at[0, core * NZ + o],
+            l1_s.at[o],
+            l_r.at[0, o],
+            at(x, zpeer(1), core),
+        )
+
+    def l1_direct(do):
+        for d in range(4):
+            do(l1_copy(zpeer(NZ - d)))
+
 
     s_t = lax.dot_general(
         keys[...], quer[...], (((1,), (1,)), ((), ())), preferred_element_type=F32
@@ -417,13 +450,6 @@
     osnd[0] = encode(b01)
     osnd[1] = encode(b45)
 
-    me = core * NZ + z
-
-    def l_copy(lvl, src, o, frm):
-        return rcopy(
-            src, lbuf.at[lvl, core * NZ + frm], l_s.at[lvl, o], l_r.at[lvl, frm], at(x, o, core)
-        )
-
     def sib_copy(lvl, o):
         dst = lbuf.at[lvl, core * NZ + o]
         return rcopy(dst, dst, sib_s.at[lvl, o], sib_r.at[lvl, o], sib)
@@ -541,22 +567,27 @@
     l3_own(lambda c: c().start())
     l2_own(lambda c: c().start())
 
-    def l1_copy(o):
-        return rcopy(
-            p1s.at[o],
-            lbuf.at[0, core * NZ + o],
-            l_s.at[0, o],
-            l_r.at[0, o],
-            at(x, zpeer(1), core),
-        )
-
-    def send_l1(o, _):
-        l1_copy(o).start()
-        return 0
+    def l1_owner(do):
+        for d in (1, 2, 3):
+            to = zpeer(NZ - d)
+
+            @pl.when(lax.rem(to, 2) == 1)
+            def _(to=to):
+                do(
+                    lambda: l_copy(
+                        0, p1r.at[lax.rem(to + NZ - 1, NZ)], to, z
+                    )
+                )
 
     @pl.when(lax.rem(z, 2) == 0)
     def _():
-        lax.fori_loop(0, NZ, send_l1, 0)
+        l1_direct(lambda c: c.start())
+
+    l1_owner(lambda c: c().start())
+
+    @pl.when(lax.rem(z, 2) == 1)
+    def _():
+        keep(0, p1r[jnp.maximum(z - 1, 0)])
 
     @pl.when(z >= 4)
     def _():
@@ -609,10 +640,10 @@
     lax.fori_loop(0, NB, gate_block, 0)
 
     def wait_e2(n, _):
-        e_copy((1 - core) * (NB // 2) + n).wait_recv()
+        e_copy((1 - core) * (NPB // 2) + n).wait_recv()
         return 0
 
-    lax.fori_loop(0, NB // 2, wait_e2, 0)
+    lax.fori_loop(0, NPB // 2, wait_e2, 0)
 
     @pl.when(core == 1)
     def _():
@@ -635,8 +666,6 @@
         to = zpeer(d)
         return rcopy(dst, dst, r_s.at[to], l_r.at[lvl, frm], at(x, to, core))
 
-    z_odd = lax.rem(z, 2) == 1
-
     def up_copy(src, frm):
         return rcopy(
             src, lbuf.at[4, core * NZ + frm], up_s.at[frm], l_r.at[4, frm], at(xpeer(1), z, core)
@@ -658,17 +687,10 @@
         arrived(zpeer(6))
         r_copy(lvl, 1, zpeer(6)).start()
 
-        @pl.when(jnp.logical_not(z_odd))
-        def _():
-            r_copy(lvl, 2, zpeer(6)).start()
-
         hand_on(zpeer(6))
         arrived(zpeer(2))
         r_copy(lvl, 7, zpeer(2)).start()
-
-        @pl.when(z_odd)
-        def _():
-            r_copy(lvl, 6, zpeer(2)).start()
+        r_copy(lvl, 6, zpeer(2)).start()
 
         hand_on(zpeer(2))
         for d in (1, 7, 3, 5, 4):
@@ -716,12 +738,11 @@
 
     @pl.when(lax.rem(z, 2) == 1)
     def _():
-        def go(o, _):
-            l1_copy(o).wait_recv()
+        def go(o):
+            l_copy(0, lbuf.at[0, me], o, o).wait_recv()
             sib_copy(0, o).start()
-            return 0
-
-        lax.fori_loop(0, NZ, go, 0)
+
+        over_z(go)
 
     l3_rest()
     l2_rest()
@@ -784,7 +805,7 @@
         e_copy(i).wait_send()
         return 0
 
-    lax.fori_loop(0, NB, e_done, 0)
+    lax.fori_loop(0, NPB, e_done, 0)
     over_z(lambda o: dz_copy(o, z).wait_send())
     over_z(lambda o: p1_copy(o, z).wait_send())
     over_x(lambda o: dx_copy(o, x).wait_send())
@@ -808,16 +829,8 @@
     def spread_done(lvl):
         for d in NEAR:
             l_copy(lvl, osnd.at[4], zpeer(d), z).wait_send()
-        for d in (1, 7):
+        for d in (1, 7, 6):
             r_copy(lvl, d, z).wait_send()
-
-        @pl.when(jnp.logical_not(z_odd))
-        def _():
-            r_copy(lvl, 2, z).wait_send()
-
-        @pl.when(z_odd)
-        def _():
-            r_copy(lvl, 6, z).wait_send()
 
     pl.when(lax.rem(x, 2) == 1)(lambda: spread_done(3))
 
@@ -840,12 +853,9 @@
 
     @pl.when(lax.rem(z, 2) == 0)
     def _():
-        def go(o, _):
-            l1_copy(o).wait_send()
-            return 0
-
-        lax.fori_loop(0, NZ, go, 0)
-
+        l1_direct(lambda c: c.wait_send())
+
+    l1_owner(lambda c: c().wait_send())
     pl.when(lax.rem(z, 2) == 1)(lambda: sib_done(0))
     pl.when(bit(z, 1))(lambda: sib_done(1))
     pl.when(z >= 4)(lambda: sib_done(2))
@@ -870,7 +880,7 @@
     dma = pltpu.SemaphoreType.DMA
     return pl.pallas_call(
         kernel,
-        out_shape=jax.ShapeDtypeStruct((TOK, WIDTH), BF16),
+        out_shape=pltpu.VMEM((TOK, WIDTH), BF16),
         in_specs=[hbm, hbm, vmem, hbm] + [vmem] * 3 + [smem] * 2,
         out_specs=vmem,
         scratch_shapes=[
@@ -907,8 +917,8 @@
             dma,
             dma,
             dma,
-            dma((NB,)),
-            dma((NB,)),
+            dma((NPB,)),
+            dma((NPB,)),
             dma((NZ,)),
             dma((NZ,)),
             dma((NX,)),
@@ -917,6 +927,7 @@
             dma((NZ,)),
             dma((5, NZ)),
             dma((5, NZ)),
+            dma((NZ,)),
             dma((NZ,)),
             dma((2, NZ)),
             dma((NZ,)),

time: 64.5 us -> 59.1 us (0.916)
  Pallas kernels: 61.8 us -> 57.9 us
  local copies, waits for them, and re-layouts: 2.46 us -> 1.06 us
    pallas_call x1, Pallas kernels: 61.8 us -> 57.9 us  [per_device(): pl.pallas_call(kernel, out_shape=pltpu.VMEM((TOK, WIDTH), BF16), in_specs...]
    unnamed x1, local copies, waits for them, and re-layouts: 2.46 us -> 1.06 us
where the time goes in v4:
time: 59.1 us; the launch traced here: 59 us
  Pallas kernels  57.9 us (98%)
  local copies, waits for them, and re-layouts  1.06 us (2%)
    pallas_call x1, Pallas kernels, per_device(): pl.pallas_call(kernel, out_shape=pltpu.VMEM((TOK, WIDTH), BF16), in_specs...  57.9 us

profile of v4, /device:TPU:238, one launch (start us, length us, event | category | flops | bytes accessed | tf_op | source)
XLA Modules:
  0.0 59.0 jit_solution(11209778005232363949)
XLA Ops:
  0.0 57.9 %layer.1 = bf16[256,2560]{1,0:T(8,128)(2,1)S(1)} custom-call(bf16[256,2816]{1,0:T(8,128)(2,1)} %mixed_h.1, bf16[256,2560]{1,0:T(8,128)(2,1)} %gate_h.1, f32[40,256]{1,0:T(8,128)} %ld.1, f32[20,40,256]{2,1,0:T(8,128)} %bitcast.1, f32[4,2816]{1,0:T(4,128)} %cw.1, f32[2816]{0:T(1024)} %cb.1, f32[2560]{0:T(1024)} %ng.1, f32[40]{0:T(128)} %skip.1, s32[3]{0:T(128)} %segl.1), custom_call_target="tpu_custom_call" | custom-call | tf_op jit(solution)/shard_map/layer/pallas_call | solution.py:881
  57.9 1.1 %copy.11 = bf16[256,2560]{1,0:T(8,128)(2,1)} copy(bf16[256,2560]{1,0:T(8,128)(2,1)S(1)} %layer.1) | data formatting | bytes 2621440

commit v5 on v4

--- a/solution.py
+++ b/solution.py
@@ -499,7 +499,7 @@
                 l3_on(1, o, mir(6)).start()
                 sib_copy(2, o).start()
 
-    def l3_rest():
+    def l3_middle():
         @pl.when(l3_mid)
         def _():
             for q in (6, 7, 0, 1):
@@ -507,6 +507,10 @@
                 l3_in(o)
                 l3_on(0, o, mir(4)).start()
                 sib_copy(2, o).start()
+
+    def l3_rest():
+        @pl.when(l3_mid)
+        def _():
             for q in (4, 3, 2):
                 o = mir(q)
                 l3_in(o)
@@ -671,7 +675,7 @@
             src, lbuf.at[4, core * NZ + frm], up_s.at[frm], l_r.at[4, frm], at(xpeer(1), z, core)
         )
 
-    def gather(lvl, up):
+    def gather(lvl, up, first):
         def arrived(frm):
             l_copy(lvl, lbuf.at[lvl, me], frm, frm).wait_recv()
 
@@ -684,6 +688,10 @@
             arrived(zpeer(d))
             hand_on(zpeer(d))
 
+        if not first:
+            for d in (1, 7, 3, 5, 4):
+                pull(d)
+            return
         arrived(zpeer(6))
         r_copy(lvl, 1, zpeer(6)).start()
 
@@ -693,8 +701,6 @@
         r_copy(lvl, 6, zpeer(2)).start()
 
         hand_on(zpeer(2))
-        for d in (1, 7, 3, 5, 4):
-            pull(d)
 
     def send_l4(frm):
         spread(3, tr.at[frm])
@@ -730,11 +736,21 @@
 
     @pl.when(lax.rem(x, 2) == 1)
     def _():
-        gather(3, False)
+        gather(3, False, True)
 
     @pl.when(x == 2)
     def _():
-        gather(4, True)
+        gather(4, True, True)
+
+    l3_middle()
+
+    @pl.when(lax.rem(x, 2) == 1)
+    def _():
+        gather(3, False, False)
+
+    @pl.when(x == 2)
+    def _():
+        gather(4, True, False)
 
     @pl.when(lax.rem(z, 2) == 1)
     def _():

time: 59.1 us -> 55.5 us (0.939); the launches traced: 59 us -> 54.7 us
  Pallas kernels: 57.9 us -> 53.7 us
    pallas_call x1, Pallas kernels: 57.9 us -> 53.7 us  [per_device(): pl.pallas_call(kernel, out_shape=pltpu.VMEM((TOK, WIDTH), BF16), in_specs...]
where the time goes in v5:
time: 55.5 us; the launch traced here: 54.7 us
  Pallas kernels  53.7 us (97%)
  local copies, waits for them, and re-layouts  1.06 us (2%)
    pallas_call x1, Pallas kernels, per_device(): pl.pallas_call(kernel, out_shape=pltpu.VMEM((TOK, WIDTH), BF16), in_specs...  53.7 us

profile of v5, /device:TPU:238, one launch (start us, length us, event | category | flops | bytes accessed | tf_op | source)
XLA Modules:
  0.0 54.7 jit_solution(16881911741428380400)
XLA Ops:
  0.0 53.7 %layer.1 = bf16[256,2560]{1,0:T(8,128)(2,1)S(1)} custom-call(bf16[256,2816]{1,0:T(8,128)(2,1)} %mixed_h.1, bf16[256,2560]{1,0:T(8,128)(2,1)} %gate_h.1, f32[40,256]{1,0:T(8,128)} %ld.1, f32[20,40,256]{2,1,0:T(8,128)} %bitcast.1, f32[4,2816]{1,0:T(4,128)} %cw.1, f32[2816]{0:T(1024)} %cb.1, f32[2560]{0:T(1024)} %ng.1, f32[40]{0:T(128)} %skip.1, s32[3]{0:T(128)} %segl.1), custom_call_target="tpu_custom_call" | custom-call | tf_op jit(solution)/shard_map/layer/pallas_call | solution.py:897
  53.7 1.1 %copy.11 = bf16[256,2560]{1,0:T(8,128)(2,1)} copy(bf16[256,2560]{1,0:T(8,128)(2,1)S(1)} %layer.1) | data formatting | bytes 2621440

commit v6 on v5

--- a/solution.py
+++ b/solution.py
@@ -659,7 +659,7 @@
     def x_in(frm):
         x_copy(frm, frm).wait_recv()
 
-    NEAR = (2, 6, 1, 7)
+    NEAR = (6, 2, 7, 1)
 
     def spread(lvl, src):
         for d in NEAR:
@@ -692,15 +692,13 @@
             for d in (1, 7, 3, 5, 4):
                 pull(d)
             return
+        arrived(zpeer(2))
+        r_copy(lvl, 6, zpeer(2)).start()
+        r_copy(lvl, 7, zpeer(2)).start()
+        hand_on(zpeer(2))
         arrived(zpeer(6))
         r_copy(lvl, 1, zpeer(6)).start()
-
         hand_on(zpeer(6))
-        arrived(zpeer(2))
-        r_copy(lvl, 7, zpeer(2)).start()
-        r_copy(lvl, 6, zpeer(2)).start()
-
-        hand_on(zpeer(2))
 
     def send_l4(frm):
         spread(3, tr.at[frm])

time: 55.5 us -> 55.2 us (level); the launches traced: 54.7 us -> 55.1 us
  no operation moved by 1% of the time
where the time goes in v6:
time: 55.2 us; the launch traced here: 55.1 us
  Pallas kernels  54 us (98%)
  local copies, waits for them, and re-layouts  1.06 us (2%)
    pallas_call x1, Pallas kernels, per_device(): pl.pallas_call(kernel, out_shape=pltpu.VMEM((TOK, WIDTH), BF16), in_specs...  54 us

profile of v6, /device:TPU:238, one launch (start us, length us, event | category | flops | bytes accessed | tf_op | source)
XLA Modules:
  0.0 55.1 jit_solution(13313339297270464763)
XLA Ops:
  0.0 54.0 %layer.1 = bf16[256,2560]{1,0:T(8,128)(2,1)S(1)} custom-call(bf16[256,2816]{1,0:T(8,128)(2,1)} %mixed_h.1, bf16[256,2560]{1,0:T(8,128)(2,1)} %gate_h.1, f32[40,256]{1,0:T(8,128)} %ld.1, f32[20,40,256]{2,1,0:T(8,128)} %bitcast.1, f32[4,2816]{1,0:T(4,128)} %cw.1, f32[2816]{0:T(1024)} %cb.1, f32[2560]{0:T(1024)} %ng.1, f32[40]{0:T(128)} %skip.1, s32[3]{0:T(128)} %segl.1), custom_call_target="tpu_custom_call" | custom-call | tf_op jit(solution)/shard_map/layer/pallas_call | solution.py:895
  54.1 1.1 %copy.11 = bf16[256,2560]{1,0:T(8,128)(2,1)} copy(bf16[256,2560]{1,0:T(8,128)(2,1)S(1)} %layer.1) | data formatting | bytes 2621440
